TPU v7x, 1024 devices: a whole 4x4x32 slice. The times are simulated.
1024 devices in a mesh: gx: 32 (over y, z_hi, x), gy: 16 (over z_lo), ta: 2 (over core).
Axes of the slice: x: 4, y: 4, z: 32 (z_hi: 2, z_lo: 16; z = z_hi * 16 + z_lo), core: 2. Of those that a mesh axis runs over, the one named last changes fastest.
Arguments:
- residual: float32 [8192, 64], P(('gx', 'gy', 'ta')), may hold values from -6 to 6
- fine_ops: bfloat16 [8192, 64, 512], P(('gx', 'gy', 'ta')), as said below
- neighbours: int32 [8192, 6], P(('gx', 'gy', 'ta')), may hold values from 0 to 7
- fine_map: int32 [8192], P(('gx', 'gy', 'ta')), may hold values from 0 to 7, as said below
- coarse_maps: int32 [1024, 3, 8], P(('gx', 'gy', 'ta')), may hold values from 0 to 7, as said below
Outputs:
- correction: float32 [8192, 64], P(('gx', 'gy', 'ta'))
Inputs may be any that keep to these rules, and one draw needn't show every extreme that they name: `fine_ops`: slot 0 of every block row is its diagonal block, whose diagonal entries are positive. `fine_map`: gives each fine block its coarse block in the level-0 node (the two devices of one ta index whose gx+gy indices differ only in bit 0); over such a pair each value is taken by exactly 2 blocks. `coarse_maps`: row l of a device maps the coarse blocks of its level-l node (the 2 ** (l + 1) devices of one ta index whose gx+gy indices agree above bit l) to those of the level-(l + 1) node; the row is the same on all devices of the level-l node, and over the two level-l nodes of one parent each value is taken exactly twice.
All inputs are finite; a program needn't handle non-finite values.
Results may differ from a plain program's by a relative error of at most 0.0019.
Values may be sent and summed in bfloat16 or wider, within the bound.
No kernel may reach another device: no remote copies, remote signals or barrier semaphores. Data moves between devices by JAX's collectives and lax.ppermute only.
A program may use at most 32 MiB of HBM per device.

v0:
```python
import jax
import jax.numpy as jnp
from jax import lax
from jax.sharding import PartitionSpec as P

BLOCK = 64
SLOTS = 8
NEIGHB = 6
COARSE = 8
LEVELS = 4
NEWTON = 4
FINE_BLOCKS = 8


exact_mode = lax.Precision.HIGHEST


def passed_along(value, axis, steps):
    count = lax.axis_size(axis)
    first, last = (max(0, -steps), min(count, count - steps))
    return lax.ppermute(value, axis, [(source, source + steps) for source in range(first, last)])


def swapped(x, axis, distance):
    return lax.ppermute(x, axis, [(i, i ^ 1 << distance) for i in range(lax.axis_size(axis))])


def newton(blocks):
    width = blocks.shape[-1]
    identity = jnp.eye(width, dtype=blocks.dtype)
    scaling = jnp.mean(jnp.diagonal(blocks, axis1=-2, axis2=-1), axis=-1)
    approx = identity * (1.0 / scaling)[..., None, None]
    for repeat in range(NEWTON):
        product = jnp.matmul(blocks, approx, precision=exact_mode)
        approx = jnp.matmul(approx, 2.0 * identity - product, precision=exact_mode)
    return approx


def one_hot(labels, classes, out_type):
    return (labels[..., None] == jnp.arange(classes, dtype=jnp.int32)).astype(out_type)


def diag_blocks(coarse_tile):
    shaped = coarse_tile.reshape(COARSE, BLOCK, COARSE, BLOCK)
    return jnp.moveaxis(jnp.diagonal(shaped, axis1=0, axis2=2), -1, 0)


def coarsen(coarse_tile, maps_now):
    select = one_hot(maps_now, COARSE, jnp.float32)
    shaped = coarse_tile.reshape(COARSE, BLOCK, COARSE, BLOCK)
    left_side = jnp.einsum("paqb,px->xaqb", shaped, select, precision=exact_mode)
    both_sides = jnp.einsum("xaqb,qy->xayb", left_side, select, precision=exact_mode)
    return both_sides.reshape(COARSE * BLOCK, COARSE * BLOCK)


def restrict_rows(values, maps_now):
    return jnp.einsum(
        "px,pa->xa", one_hot(maps_now, COARSE, jnp.float32), values, precision=exact_mode
    )


def apply_tile(coarse_tile, values):
    return jnp.dot(coarse_tile, values.reshape(-1), precision=exact_mode).reshape(COARSE, BLOCK)


def smooth_blocks(blocks, coarse_rows):
    inverse = newton(blocks)
    return jnp.einsum("pab,pb->pa", inverse, coarse_rows, precision=exact_mode)


def coarse_smooth(coarse_tile, coarse_rows):
    return smooth_blocks(diag_blocks(coarse_tile), coarse_rows)


def on_device(residual, fine_ops, neighbours, fine_map, coarse_maps):
    diagonal_part = fine_ops[:, :, :BLOCK].astype(jnp.float32)
    fine_smooth = jnp.einsum("nab,nb->na", newton(diagonal_part), residual, precision=exact_mode)
    rounded = fine_smooth.astype(jnp.bfloat16)
    earlier = passed_along(rounded, "ta", 1)
    nearby = rounded[neighbours]
    stacked = jnp.concatenate([rounded[:, None], nearby, earlier[:, None]], axis=1)
    stacked = stacked.reshape(FINE_BLOCKS, SLOTS * BLOCK)
    applied = jnp.einsum("nam,nm->na", fine_ops, stacked, preferred_element_type=jnp.float32)
    fine_resid = residual - applied
    targets = jnp.concatenate([fine_map[:, None], fine_map[neighbours]], axis=1)
    select = one_hot(fine_map, COARSE, jnp.float32)
    target_hot = one_hot(targets, COARSE, jnp.float32)
    combined = jnp.einsum("np,nkq->pqnk", select, target_hot).astype(jnp.bfloat16)
    spatial = fine_ops[:, :, : (NEIGHB + 1) * BLOCK].reshape(FINE_BLOCKS, BLOCK, NEIGHB + 1, BLOCK)
    first_tile = jnp.einsum(
        "pqnk,nakb->paqb", combined, spatial, preferred_element_type=jnp.float32
    )
    first_tile = first_tile.reshape(COARSE * BLOCK, COARSE * BLOCK)
    first_rows = jnp.einsum("np,na->pa", select, fine_resid, precision=exact_mode)
    level_maps = coarse_maps[0]
    level_vals = []
    current_tile = first_tile
    current_rows = first_rows
    for section_num in range(LEVELS):
        other_tile, other_rows = swapped((current_tile, current_rows), ("gx", "gy"), section_num)
        current_tile = current_tile + other_tile
        current_rows = current_rows + other_rows
        smoothed = coarse_smooth(current_tile, current_rows)
        level_vals.append(smoothed)
        if section_num < LEVELS - 1:
            leftover = current_rows - apply_tile(current_tile, smoothed)
            current_tile = coarsen(current_tile, level_maps[section_num])
            current_rows = restrict_rows(leftover, level_maps[section_num])
    correction_now = level_vals[-1]
    for section_num in range(LEVELS - 2, -1, -1):
        spread = one_hot(level_maps[section_num], COARSE, jnp.float32)
        correction_now = level_vals[section_num] + jnp.einsum(
            "px,xa->pa", spread, correction_now, precision=exact_mode
        )
    fine_part = jnp.einsum("nx,xa->na", select, correction_now, precision=exact_mode)
    return fine_smooth + fine_part


def solution(mesh):
    return jax.shard_map(
        on_device,
        mesh=mesh,
        in_specs=(
            P(("gx", "gy", "ta"), None),
            P(("gx", "gy", "ta"), None, None),
            P(("gx", "gy", "ta"), None),
            P(("gx", "gy", "ta")),
            P(("gx", "gy", "ta"), None, None),
        ),
        out_specs=P(("gx", "gy", "ta"), None),
        check_vma=False,
    )
```

profile of v0, /device:TPU:1, one launch (start us, length us, event | category | flops | bytes accessed | tf_op | source)
XLA Modules:
  0.0 432.7 jit_solution(8619510916388208712)
XLA Ops:
  10.3 2.1 convolution_bitcast_fusion
  12.5 1.9 reshape.93
  14.4 4.4 %collective-permute-start = (f32[512,512]{1,0:T(8,128)S(1)}, f32[512,512]{1,0:T(8,128)S(1)}, u32[]{:S(2)}, u32[]{:S(2)}) collective-permute-start(f32[512,512]{1,0:T(8,128)S(1)} %reshape.93), channel_id=1, source_target_pairs={{0,2},{2,0},{4,6},{6,4},{8,10},{10,8},{12,14},{14,12},{16,18},{18,... | collective-permute-start | bytes 3145736 | tf_op jit(solution)/shard_map/ppermute | solution.py:25
  19.5 3.7 collective-permute-done.1
  23.7 2.4 collective-permute-start.2
  26.1 4.9 %collective-permute-done.2 = f32[8,64]{1,0:T(8,128)S(1)} collective-permute-done((f32[8,64]{1,0:T(8,128)S(1)}, f32[8,64]{1,0:T(8,128)S(1)}, u32[]{:S(2)}, u32[]{:S(2)}) %collective-permute-start.2) | collective-permute-done | bytes 2080 | tf_op jit(solution)/shard_map/ppermute | solution.py:25
  31.7 1.7 copy.171
  33.4 2.2 gather_fusion.2
  35.5 2.0 copy.35
  43.3 2.2 fusion.10
  48.3 15.2 %collective-permute-start.3 = (f32[512,512]{1,0:T(8,128)}, f32[512,512]{1,0:T(8,128)S(1)}, u32[]{:S(2)}, u32[]{:S(2)}) collective-permute-start(f32[512,512]{1,0:T(8,128)} %reshape.96), channel_id=1, source_target_pairs={{0,4},{2,6},{4,0},{6,2},{8,12},{10,14},{12,8},{14,10},{16,20},{18,... | collective-permute-start | bytes 3145736 | tf_op jit(solution)/shard_map/ppermute | solution.py:25
  63.5 1.5 convolution_subtract_fusion.12
  68.6 2.1 collective-permute-start.4
  70.7 38.2 %collective-permute-done.4 = f32[8,64]{1,0:T(8,128)S(1)} collective-permute-done((f32[8,64]{1,0:T(8,128)S(1)}, f32[8,64]{1,0:T(8,128)S(1)}, u32[]{:S(2)}, u32[]{:S(2)}) %collective-permute-start.4) | collective-permute-done | bytes 2080 | tf_op jit(solution)/shard_map/ppermute | solution.py:25
  109.6 1.7 copy.170
  111.3 2.2 gather_fusion.5
  113.5 2.0 copy.49
  121.3 2.2 fusion.6
  126.3 8.9 %collective-permute-start.5 = (f32[512,512]{1,0:T(8,128)}, f32[512,512]{1,0:T(8,128)S(1)}, u32[]{:S(2)}, u32[]{:S(2)}) collective-permute-start(f32[512,512]{1,0:T(8,128)} %reshape.99), channel_id=1, source_target_pairs={{0,8},{2,10},{4,12},{6,14},{8,0},{10,2},{12,4},{14,6},{16,24},{18,... | collective-permute-start | bytes 3145736 | tf_op jit(solution)/shard_map/ppermute | solution.py:25
  135.2 1.5 convolution_subtract_fusion.8
  140.3 2.1 collective-permute-start.6
  142.5 83.3 %collective-permute-done.6 = f32[8,64]{1,0:T(8,128)S(1)} collective-permute-done((f32[8,64]{1,0:T(8,128)S(1)}, f32[8,64]{1,0:T(8,128)S(1)}, u32[]{:S(2)}, u32[]{:S(2)}) %collective-permute-start.6) | collective-permute-done | bytes 2080 | tf_op jit(solution)/shard_map/ppermute | solution.py:25
  226.4 1.7 copy.169
  228.2 2.2 gather_fusion.7
  230.3 2.0 copy.61
  238.1 2.2 fusion.2
  243.1 83.4 %collective-permute-start.7 = (f32[512,512]{1,0:T(8,128)}, f32[512,512]{1,0:T(8,128)S(1)}, u32[]{:S(2)}, u32[]{:S(2)}) collective-permute-start(f32[512,512]{1,0:T(8,128)} %reshape.102), channel_id=1, source_target_pairs={{0,16},{2,18},{4,20},{6,22},{8,24},{10,26},{12,28},{14,30},{16,0},... | collective-permute-start | bytes 3145736 | tf_op jit(solution)/shard_map/ppermute | solution.py:25
  326.5 1.5 convolution_subtract_fusion.4
  331.6 2.2 collective-permute-start.8
  333.8 85.7 %collective-permute-done.8 = f32[8,64]{1,0:T(8,128)S(1)} collective-permute-done((f32[8,64]{1,0:T(8,128)S(1)}, f32[8,64]{1,0:T(8,128)S(1)}, u32[]{:S(2)}, u32[]{:S(2)}) %collective-permute-start.8) | collective-permute-done | bytes 2080 | tf_op jit(solution)/shard_map/ppermute | solution.py:25
  419.8 1.8 reshape.103
  421.5 2.0 copy.168
  (139 shorter events, 58.4 us)
Async XLA Ops:
  0.0 2.6 copy-start.4
  3.7 2.9 copy-start.5
  4.1 4.3 copy-start.6
  4.1 4.4 %copy-start = (s32[8]{0:T(128)S(1)}, s32[8]{0:T(128)}, u32[]{:S(2)}) copy-start(s32[8]{0:T(128)} %param.8) | copy-start | bytes 100
  7.1 16.0 %collective-permute-start.1 = (bf16[8,64]{1,0:T(8,128)(2,1)S(1)}, bf16[8,64]{1,0:T(8,128)(2,1)S(1)}, u32[]{:S(2)}, u32[]{:S(2)}) collective-permute-start(bf16[8,64]{1,0:T(8,128)(2,1)S(1)} %convert_element_type.46), channel_id=1, source_target_pairs={{0,1},{2,3},{4,5},{6,7},{8,9},{10,11},{12,13},{14,15},{16,17},{18,... | collective-permute-start | bytes 3080 | tf_op jit(solution)/shard_map/ppermute | solution.py:21
  12.5 6.3 %copy-start.7 = (s32[1,3,8]{2,0,1:T(1,128)S(1)}, s32[1,3,8]{2,0,1:T(1,128)}, u32[]{:S(2)}) copy-start(s32[1,3,8]{2,0,1:T(1,128)} %param.9) | copy-start | bytes 292
  14.4 16.6 %collective-permute-start = (f32[512,512]{1,0:T(8,128)S(1)}, f32[512,512]{1,0:T(8,128)S(1)}, u32[]{:S(2)}, u32[]{:S(2)}) collective-permute-start(f32[512,512]{1,0:T(8,128)S(1)} %reshape.93), channel_id=1, source_target_pairs={{0,2},{2,0},{4,6},{6,4},{8,10},{10,8},{12,14},{14,12},{16,18},{18,... | collective-permute-start | bytes 3145736 | tf_op jit(solution)/shard_map/ppermute | solution.py:25
  23.7 7.4 %collective-permute-start.2 = (f32[8,64]{1,0:T(8,128)S(1)}, f32[8,64]{1,0:T(8,128)S(1)}, u32[]{:S(2)}, u32[]{:S(2)}) collective-permute-start(f32[8,64]{1,0:T(8,128)S(1)} %fusion.88), channel_id=1, source_target_pairs={{0,2},{2,0},{4,6},{6,4},{8,10},{10,8},{12,14},{14,12},{16,18},{18,... | collective-permute-start | bytes 6152 | tf_op jit(solution)/shard_map/ppermute | solution.py:25
  48.3 60.7 %copy-start.1 = (f32[512,512]{1,0:T(8,128)S(1)}, f32[512,512]{1,0:T(8,128)}, u32[]{:S(2)}) copy-start(f32[512,512]{1,0:T(8,128)} %reshape.96) | copy-start | bytes 3145732
  48.3 60.7 %collective-permute-start.3 = (f32[512,512]{1,0:T(8,128)}, f32[512,512]{1,0:T(8,128)S(1)}, u32[]{:S(2)}, u32[]{:S(2)}) collective-permute-start(f32[512,512]{1,0:T(8,128)} %reshape.96), channel_id=1, source_target_pairs={{0,4},{2,6},{4,0},{6,2},{8,12},{10,14},{12,8},{14,10},{16,20},{18,... | collective-permute-start | bytes 3145736 | tf_op jit(solution)/shard_map/ppermute | solution.py:25
  68.6 40.3 %collective-permute-start.4 = (f32[8,64]{1,0:T(8,128)S(1)}, f32[8,64]{1,0:T(8,128)S(1)}, u32[]{:S(2)}, u32[]{:S(2)}) collective-permute-start(f32[8,64]{1,0:T(8,128)S(1)} %fusion.83), channel_id=1, source_target_pairs={{0,4},{2,6},{4,0},{6,2},{8,12},{10,14},{12,8},{14,10},{16,20},{18,... | collective-permute-start | bytes 6152 | tf_op jit(solution)/shard_map/ppermute | solution.py:25
  126.3 99.5 %copy-start.2 = (f32[512,512]{1,0:T(8,128)S(1)}, f32[512,512]{1,0:T(8,128)}, u32[]{:S(2)}) copy-start(f32[512,512]{1,0:T(8,128)} %reshape.99) | copy-start | bytes 3145732
  126.3 99.5 %collective-permute-start.5 = (f32[512,512]{1,0:T(8,128)}, f32[512,512]{1,0:T(8,128)S(1)}, u32[]{:S(2)}, u32[]{:S(2)}) collective-permute-start(f32[512,512]{1,0:T(8,128)} %reshape.99), channel_id=1, source_target_pairs={{0,8},{2,10},{4,12},{6,14},{8,0},{10,2},{12,4},{14,6},{16,24},{18,... | collective-permute-start | bytes 3145736 | tf_op jit(solution)/shard_map/ppermute | solution.py:25
  140.3 85.5 %collective-permute-start.6 = (f32[8,64]{1,0:T(8,128)S(1)}, f32[8,64]{1,0:T(8,128)S(1)}, u32[]{:S(2)}, u32[]{:S(2)}) collective-permute-start(f32[8,64]{1,0:T(8,128)S(1)} %fusion.78), channel_id=1, source_target_pairs={{0,8},{2,10},{4,12},{6,14},{8,0},{10,2},{12,4},{14,6},{16,24},{18,... | collective-permute-start | bytes 6152 | tf_op jit(solution)/shard_map/ppermute | solution.py:25
  243.1 176.5 %copy-start.3 = (f32[512,512]{1,0:T(8,128)S(1)}, f32[512,512]{1,0:T(8,128)}, u32[]{:S(2)}) copy-start(f32[512,512]{1,0:T(8,128)} %reshape.102) | copy-start | bytes 3145732
  243.1 176.4 %collective-permute-start.7 = (f32[512,512]{1,0:T(8,128)}, f32[512,512]{1,0:T(8,128)S(1)}, u32[]{:S(2)}, u32[]{:S(2)}) collective-permute-start(f32[512,512]{1,0:T(8,128)} %reshape.102), channel_id=1, source_target_pairs={{0,16},{2,18},{4,20},{6,22},{8,24},{10,26},{12,28},{14,30},{16,0},... | collective-permute-start | bytes 3145736 | tf_op jit(solution)/shard_map/ppermute | solution.py:25
  331.6 87.9 %collective-permute-start.8 = (f32[8,64]{1,0:T(8,128)S(1)}, f32[8,64]{1,0:T(8,128)S(1)}, u32[]{:S(2)}, u32[]{:S(2)}) collective-permute-start(f32[8,64]{1,0:T(8,128)S(1)} %fusion.73), channel_id=1, source_target_pairs={{0,16},{2,18},{4,20},{6,22},{8,24},{10,26},{12,28},{14,30},{16,0},... | collective-permute-start | bytes 6152 | tf_op jit(solution)/shard_map/ppermute | solution.py:25
where the time goes:
time: 439 us; the launch traced here: 433 us
  waiting for transfers between devices  216 us (49%)
  starting transfers between devices  122 us (28%)
  matrix products  51.9 us (12%)
  local copies, waits for them, and re-layouts  39.7 us (9%)
    ppermute x8, waiting for transfers between devices, swapped(): lax.ppermute(x, axis, [(i, i ^ 1 << distance) for i in range(lax.axis_siz...  212 us
    ppermute x8, starting transfers between devices, swapped(): lax.ppermute(x, axis, [(i, i ^ 1 << distance) for i in range(lax.axis_siz...  121 us
    dot_general x20, matrix products, newton(): approx = jnp.matmul(approx, 2.0 * identity - product, precision=exact_mode)  16.1 us
    dot_general x20, matrix products, newton(): product = jnp.matmul(blocks, approx, precision=exact_mode)  14.4 us
    gather x8, local copies, waits for them, and re-layouts, diag_blocks(): return jnp.moveaxis(jnp.diagonal(shaped, axis1=0, axis2=2), -1, 0)  13.6 us
    reshape x8, local copies, waits for them, and re-layouts, diag_blocks(): shaped = coarse_tile.reshape(COARSE, BLOCK, COARSE, BLOCK)  10.1 us
  transfers between devices with their start and end apart: 9, of which 5 were waited for; matrix products, arithmetic and copies ran while one was open for 5% of the time, Pallas kernels for 0%

commit v1 on v0

v1 whole, which is shorter than its diff:
```python
import jax
import jax.numpy as jnp
from jax import lax
from jax.experimental import pallas as pl
from jax.experimental.pallas import tpu as pltpu
from jax.sharding import PartitionSpec as P

BLOCK = 64
SLOTS = 8
NEIGHB = 6
COARSE = 8
LEVELS = 4
FINE_BLOCKS = 8
PAIRS = COARSE // 2
WIDE = 2 * BLOCK
ROWS = COARSE
INTERPRET = False

F32 = jnp.float32
BF16 = jnp.bfloat16
I32 = jnp.int32


def iota(shape, axis):
    return lax.broadcasted_iota(I32, shape, axis)


def product(x, weights):
    return jnp.dot(x, weights, preferred_element_type=F32)


def product_nt(x, weights):
    return lax.dot_general(x, weights, (((1,), (1,)), ((), ())), preferred_element_type=F32)


def split(x):
    high = x.astype(BF16)
    return high, (x - high.astype(F32)).astype(BF16)


def split_rows(x):
    high = x.astype(BF16).astype(F32)
    return jnp.concatenate([high, x - high], axis=0).astype(BF16)


def twice(x):
    return jnp.concatenate([x, x], axis=1)


def own_lanes(pair):
    return iota((ROWS, WIDE), 0) == 2 * pair + iota((ROWS, WIDE), 1) // BLOCK


def spread(values):
    doubled = twice(values)
    return jnp.concatenate([jnp.where(own_lanes(q), doubled, 0.0) for q in range(PAIRS)], axis=1)


def fold(wide):
    kept = sum(jnp.where(own_lanes(q), wide[:, q * WIDE : (q + 1) * WIDE], 0.0) for q in range(PAIRS))
    return kept[:, :BLOCK] + kept[:, BLOCK:]


def squared(error):
    left = (iota((BLOCK, WIDE), 1) < BLOCK).astype(F32).astype(BF16)
    right = (iota((BLOCK, WIDE), 1) >= BLOCK).astype(F32).astype(BF16)
    high, low = split(error)
    weights = jnp.concatenate(
        [
            jnp.concatenate([high * left, high * right], axis=0),
            jnp.concatenate([low * left, low * right], axis=0),
        ],
        axis=1,
    )
    full = product(jnp.concatenate([high, low], axis=0), weights)
    top = full[:BLOCK] + full[BLOCK:]
    return top[:, :WIDE] + top[:, WIDE:]


def operand(errors):
    parts = [split(one) for one in errors]
    return jnp.concatenate(
        [jnp.concatenate([h for h, _ in parts], axis=1), jnp.concatenate([l for _, l in parts], axis=1)],
        axis=0,
    )


def applied(weights, values):
    full = product_nt(split_rows(spread(values)), weights)
    top = full[:ROWS] + full[ROWS:]
    return top[:, :BLOCK] + top[:, BLOCK:]


def smooth(pairs, values):
    eye = iota((BLOCK, WIDE), 0) == iota((BLOCK, WIDE), 1) % BLOCK
    sums = sum(
        jnp.where(own_lanes(q), jnp.sum(jnp.where(eye, pairs[q], 0.0), axis=0, keepdims=True), 0.0)
        for q in range(PAIRS)
    )
    inverse = 1.0 / (jnp.sum(sums, axis=1, keepdims=True) * (1.0 / BLOCK))
    one = eye.astype(F32)
    first = []
    for q in range(PAIRS):
        along = jnp.sum(jnp.where(own_lanes(q), inverse, 0.0), axis=0, keepdims=True)
        first.append(one - pairs[q] * along)
    second = [squared(e) for e in first]
    fourth = [squared(e) for e in second]
    w1, w2, w4 = operand(first), operand(second), operand(fourth)
    y = values
    y = y + applied(w4, applied(w4, y))
    y = y + applied(w4, y)
    y = y + applied(w2, y)
    y = y + applied(w1, y)
    return y * inverse


def picked(index, values):
    return sum(jnp.where(index == x, values[x : x + 1], 0.0) for x in range(COARSE))


def restricted(index, values):
    total = jnp.zeros_like(values)
    for x in range(COARSE):
        row = jnp.sum(jnp.where(index == x, values, 0.0), axis=0, keepdims=True)
        total = total + jnp.where(iota(values.shape, 0) == x, row, 0.0)
    return total


def gathered(maps_ref, doubled):
    return [picked(maps_ref[q], doubled) for q in range(PAIRS)]


def ops_product(ops_ref, tiles):
    stacked = split_rows(jnp.concatenate(tiles, axis=1))
    full = product_nt(stacked, ops_ref[...])
    return fold(full[:ROWS] + full[ROWS:])


def fine_kernel(ops_ref, resid_ref, smooth_ref, rounded_ref):
    pairs = []
    for q in range(PAIRS):
        even = ops_ref[2 * q * BLOCK : (2 * q + 1) * BLOCK, :BLOCK].astype(F32)
        odd = ops_ref[(2 * q + 1) * BLOCK : (2 * q + 2) * BLOCK, :BLOCK].astype(F32)
        pairs.append(jnp.concatenate([even, odd], axis=1))
    out = smooth(pairs, resid_ref[...])
    smooth_ref[...] = out
    rounded_ref[...] = out.astype(BF16)


def tiles_kernel(near_ref, fine_map_ref, maps_ref, ops_ref, cols_ref, tiles_ref, acc_ref):
    acc_ref[...] = jnp.zeros_like(acc_ref)
    left = iota((1, WIDE), 1) < BLOCK
    rows = iota((ROWS, WIDE), 0)
    first_half = iota((ROWS, WIDE), 1) < BLOCK

    def label(j, level):
        value = fine_map_ref[j]
        for step in range(level):
            value = maps_ref[0, step, value]
        return value

    index = [jnp.where(first_half, rows, -1)] + [jnp.full((ROWS, WIDE), -1, I32) for q in range(PAIRS - 1)]
    level_cols = [jnp.zeros((ROWS, WIDE), I32) for level in range(LEVELS)]
    for j in range(FINE_BLOCKS):
        own = [label(j, level) for level in range(LEVELS)]
        others = [near_ref[j, k] for k in range(NEIGHB)]
        for level in range(LEVELS):
            level_cols[level] = jnp.where(rows == j, own[level], level_cols[level])
        for k in range(1, NEIGHB + 1):
            here = (rows == j) & (first_half if k % 2 == 0 else ~first_half)
            index[k // 2] = jnp.where(here, others[k - 1], index[k // 2])
        tiles = [
            ops_ref[j * BLOCK : (j + 1) * BLOCK, q * WIDE : (q + 1) * WIDE].astype(F32) for q in range(PAIRS)
        ]
        for level in range(LEVELS):
            same = [F32(1.0)] + [
                jnp.where(label(others[k], level) == own[level], F32(1.0), F32(0.0)) for k in range(NEIGHB)
            ]
            total = None
            for q in range(PAIRS):
                odd = same[2 * q + 1] if 2 * q + 1 <= NEIGHB else F32(0.0)
                part = tiles[q] * jnp.where(left, same[2 * q], odd)
                total = part if total is None else total + part
            acc_ref[level, own[level]] = acc_ref[level, own[level]] + total
    for q in range(PAIRS):
        cols_ref[q] = index[q]
    for level in range(LEVELS):
        cols_ref[PAIRS + level] = level_cols[level]
        for q in range(PAIRS):
            even, odd = acc_ref[level, 2 * q], acc_ref[level, 2 * q + 1]
            wide_left = iota((BLOCK, WIDE), 1) < BLOCK
            moved = pltpu.roll(jnp.where(wide_left, odd, even), BLOCK, 1)
            tiles_ref[level, q] = jnp.where(wide_left, even, odd) + moved


def store_rows(out_ref, start, values):
    out_ref[start : start + ROWS, :] = twice(values)


SEND0 = ROWS + PAIRS * BLOCK + 2 * BLOCK
SEND1 = ROWS + 2 * BLOCK + BLOCK
SEND2 = ROWS + BLOCK + BLOCK // 2
SEND3 = ROWS + BLOCK // 2


def resid_kernel(ops_ref, resid_ref, rounded_ref, earlier_ref, cols_ref, tiles_ref, fresid_ref, send_ref):
    own = twice(rounded_ref[...].astype(F32))
    before = twice(earlier_ref[...].astype(F32))
    tiles = gathered(cols_ref, own)
    tiles[-1] = jnp.where(iota((ROWS, WIDE), 1) < BLOCK, tiles[-1], before)
    stacked = jnp.concatenate(tiles, axis=1)
    stacked = jnp.concatenate([stacked, jnp.zeros_like(stacked)], axis=0).astype(BF16)
    fresid = resid_ref[...] - fold(product_nt(stacked, ops_ref[...])[:ROWS])
    fresid_ref[...] = fresid
    store_rows(send_ref, 0, restricted(cols_ref[PAIRS][:, :BLOCK], fresid))
    other = 1 - lax.rem(lax.axis_index("gy"), 2)
    for q in range(PAIRS):
        send_ref[ROWS + q * BLOCK : ROWS + (q + 1) * BLOCK, :] = tiles_ref[0, q]
    at = ROWS + PAIRS * BLOCK
    for i in range(2):
        send_ref[at + i * BLOCK : at + (i + 1) * BLOCK, :] = tiles_ref[1, 2 * other + i]


def descend(level, pairs, coarse_rows, ops_ref, cols_ref, fresid_ref, total_ref, fresid_out, total_out):
    out = smooth(pairs, coarse_rows)
    on_fine = picked(cols_ref[PAIRS + level][:, :BLOCK], out)
    total_out[...] = total_ref[...] + on_fine
    fresid = fresid_ref[...] - ops_product(ops_ref, gathered(cols_ref, twice(on_fine)))
    if fresid_out is not None:
        fresid_out[...] = fresid
    return twice(restricted(cols_ref[PAIRS + level + 1][:, :BLOCK], fresid))


def level0_kernel(ops_ref, cols_ref, tiles_ref, sent_ref, got_ref, fresid_ref, total_ref, fresid_out, total_out, send_ref):
    half = lax.rem(lax.axis_index("gy"), 2)
    pairs = [
        tiles_ref[0, q] + got_ref[ROWS + q * BLOCK : ROWS + (q + 1) * BLOCK, :] for q in range(PAIRS)
    ]
    coarse_rows = sent_ref[:ROWS, :BLOCK] + got_ref[:ROWS, :BLOCK]
    at = ROWS + PAIRS * BLOCK
    summed = [tiles_ref[1, 2 * half + i] + got_ref[at + i * BLOCK : at + (i + 1) * BLOCK, :] for i in range(2)]
    rows = descend(0, pairs, coarse_rows, ops_ref, cols_ref, fresid_ref, total_ref, fresid_out, total_out)
    for e in range(4):
        base = e * SEND1
        send_ref[base : base + ROWS, :] = rows
        for i in range(2):
            send_ref[base + ROWS + i * BLOCK : base + ROWS + (i + 1) * BLOCK, :] = summed[i]
        send_ref[base + ROWS + 2 * BLOCK : base + SEND1, :] = tiles_ref[2, e]


def level1_kernel(ops_ref, cols_ref, tiles_ref, got_ref, fresid_ref, total_ref, fresid_out, total_out, send_ref):
    def chunk(e, start, size):
        return got_ref[e * SEND1 + start : e * SEND1 + start + size, :]

    coarse_rows = sum(chunk(e, 0, ROWS) for e in range(4))[:, :BLOCK]
    pairs = []
    for q in range(PAIRS):
        half, i = q // 2, q % 2
        pairs.append(chunk(half, ROWS + i * BLOCK, BLOCK) + chunk(half + 2, ROWS + i * BLOCK, BLOCK))
    summed = sum(chunk(e, ROWS + 2 * BLOCK, BLOCK) for e in range(4))
    rows = descend(1, pairs, coarse_rows, ops_ref, cols_ref, fresid_ref, total_ref, fresid_out, total_out)
    for e in range(8):
        base = e * SEND2
        send_ref[base : base + ROWS, :] = rows
        send_ref[base + ROWS : base + ROWS + BLOCK, :] = summed
        part = BLOCK // 2 * (e % 2)
        send_ref[base + ROWS + BLOCK : base + SEND2, :] = tiles_ref[3, e // 2, part : part + BLOCK // 2, :]


def level2_kernel(ops_ref, cols_ref, got_ref, fresid_ref, total_ref, total_out, send_ref):
    def chunk(e, start, size):
        return got_ref[e * SEND2 + start : e * SEND2 + start + size, :]

    coarse_rows = sum(chunk(e, 0, ROWS) for e in range(8))[:, :BLOCK]
    pairs = [chunk(q, ROWS, BLOCK) + chunk(q + 4, ROWS, BLOCK) for q in range(PAIRS)]
    summed = sum(chunk(e, ROWS + BLOCK, BLOCK // 2) for e in range(8))
    rows = descend(2, pairs, coarse_rows, ops_ref, cols_ref, fresid_ref, total_ref, None, total_out)
    for e in range(16):
        base = e * SEND3
        send_ref[base : base + ROWS, :] = rows
        send_ref[base + ROWS : base + SEND3, :] = summed


def level3_kernel(cols_ref, got_ref, total_ref, out_ref):
    def chunk(e, start, size):
        return got_ref[e * SEND3 + start : e * SEND3 + start + size, :]

    coarse_rows = sum(chunk(e, 0, ROWS) for e in range(16))[:, :BLOCK]
    eighths = [chunk(e, ROWS, BLOCK // 2) + chunk(e + 8, ROWS, BLOCK // 2) for e in range(8)]
    pairs = [jnp.concatenate([eighths[2 * q], eighths[2 * q + 1]], axis=0) for q in range(PAIRS)]
    out = smooth(pairs, coarse_rows)
    out_ref[...] = total_ref[...] + picked(cols_ref[PAIRS + 3][:, :BLOCK], out)


def call(kernel, name, out_shapes, args, scalars=0, scratch=()):
    vmem = pl.BlockSpec(memory_space=pltpu.VMEM)
    smem = pl.BlockSpec(memory_space=pltpu.SMEM)
    return pl.pallas_call(
        kernel,
        name=name,
        out_shape=[jax.ShapeDtypeStruct(shape, kind) for shape, kind in out_shapes],
        in_specs=[smem] * scalars + [vmem] * (len(args) - scalars),
        out_specs=[vmem] * len(out_shapes),
        scratch_shapes=list(scratch),
        interpret=INTERPRET,
    )(*args)


def shared(chunks, size):
    lists = [[g * size + i for i in range(size)] for g in range(lax.axis_size("gy") // size)]
    return lax.all_to_all(chunks, "gy", 0, 0, axis_index_groups=lists, tiled=True)


def on_device(residual, fine_ops, neighbours, fine_map, coarse_maps):
    ops = fine_ops.reshape(FINE_BLOCKS * BLOCK, SLOTS * BLOCK)
    vec = (FINE_BLOCKS, BLOCK)
    fine_smooth, rounded = call(fine_kernel, "fine_smooth", [(vec, F32), (vec, BF16)], [ops, residual])
    earlier = lax.ppermute(rounded, "ta", [(0, 1)])
    cols, tiles = call(
        tiles_kernel,
        "tile_parts",
        [((PAIRS + LEVELS, ROWS, WIDE), I32), ((LEVELS, PAIRS, BLOCK, WIDE), F32)],
        [neighbours, fine_map, coarse_maps, ops],
        scalars=3,
        scratch=[pltpu.VMEM((LEVELS, COARSE, BLOCK, WIDE), F32)],
    )
    fresid, sent = call(
        resid_kernel,
        "fine_resid",
        [(vec, F32), ((SEND0, WIDE), F32)],
        [ops, residual, rounded, earlier, cols, tiles],
    )
    got = lax.ppermute(sent, "gy", [(i, i ^ 1) for i in range(lax.axis_size("gy"))])
    fresid, total, chunks = call(
        level0_kernel,
        "level_0",
        [(vec, F32), (vec, F32), ((4 * SEND1, WIDE), F32)],
        [ops, cols, tiles, sent, got, fresid, fine_smooth],
    )
    got = shared(chunks, 4)
    fresid, total, chunks = call(
        level1_kernel,
        "level_1",
        [(vec, F32), (vec, F32), ((8 * SEND2, WIDE), F32)],
        [ops, cols, tiles, got, fresid, total],
    )
    got = shared(chunks, 8)
    total, chunks = call(
        level2_kernel,
        "level_2",
        [(vec, F32), ((16 * SEND3, WIDE), F32)],
        [ops, cols, got, fresid, total],
    )
    got = shared(chunks, 16)
    (out,) = call(level3_kernel, "level_3", [(vec, F32)], [cols, got, total])
    return out


def solution(mesh):
    return jax.shard_map(
        on_device,
        mesh=mesh,
        in_specs=(
            P(("gx", "gy", "ta"), None),
            P(("gx", "gy", "ta"), None, None),
            P(("gx", "gy", "ta"), None),
            P(("gx", "gy", "ta")),
            P(("gx", "gy", "ta"), None, None),
        ),
        out_specs=P(("gx", "gy", "ta"), None),
        check_vma=False,
    )
```

time: 439 us -> 142 us (0.32)
  the two profiles are of different devices: /device:TPU:1 before, /device:TPU:60 now
where the time goes in v1:
time: 142 us
  blocking collectives  104 us (73%)
  Pallas kernels  25.3 us (18%)
  waiting for transfers between devices  6.36 us (4%)
  starting transfers between devices  3.86 us (3%)
  local copies, waits for them, and re-layouts  1.85 us (1%)
    all_to_all x3, blocking collectives, shared(): lax.all_to_all(chunks, 'gy', 0, 0, axis_index_groups=lists, tiled=True)  104 us
    pallas_call x7, Pallas kernels, call(): pl.pallas_call(kernel, name=name, out_shape=[jax.ShapeDtypeStruct(shape,...  25.3 us
    ppermute x1, waiting for transfers between devices, on_device(): lax.ppermute(sent, 'gy', [(i, i ^ 1) for i in range(lax.axis_size('gy'))])  6.36 us
  transfers between devices with their start and end apart: 2, of which 1 were waited for; matrix products, arithmetic and copies ran while one was open for 0% of the time, Pallas kernels for 2%

profile of v1, /device:TPU:60, one launch (start us, length us, event | category | flops | bytes accessed | tf_op | source)
XLA Modules:
  0.0 141.7 jit_solution(10347691391664639121)
XLA Ops:
  0.0 3.6 %fine_smooth.1 = (f32[8,64]{1,0:T(8,128)}, bf16[8,64]{1,0:T(8,128)(2,1)}) custom-call(bf16[512,512]{1,0:T(8,128)(2,1)} %bitcast.7, f32[8,64]{1,0:T(8,128)} %resid_ref.3), custom_call_target="tpu_custom_call" | custom-call | tf_op jit(solution)/shard_map/fine_smooth/pallas_call | solution.py:298
  3.6 0.0 copy-start.2
  3.6 1.9 %collective-permute-start = (bf16[8,64]{1,0:T(8,128)(2,1)}, bf16[8,64]{1,0:T(8,128)(2,1)S(1)}, u32[]{:S(2)}, u32[]{:S(2)}) collective-permute-start(bf16[8,64]{1,0:T(8,128)(2,1)} %get-tuple-element.21.rounded_ref), channel_id=1, source_target_pairs={{0,1},{2,3},{4,5},{6,7},{8,9},{10,11},{12,13},{14,15},{16,17},{18,... | collective-permute-start | bytes 3080 | tf_op jit(solution)/shard_map/ppermute | solution.py:318
  5.5 0.0 copy-done.2
  5.5 0.6 copy.6.maps_ref
  6.1 2.7 %tile_parts.1 = (s32[8,8,128]{2,1,0:T(8,128)}, f32[4,4,64,128]{3,2,1,0:T(8,128)}) custom-call(s32[8,6]{1,0:T(8,128)} %near_ref.1, s32[8]{0:T(128)} %fine_map_ref.1, s32[1,3,8]{2,1,0:T(4,128)} %copy.6.maps_ref, bf16[512,512]{1,0:T(8,128)(2,1)} %bitcast.8), custom_call_target="tpu_custom_call" | custom-call | tf_op jit(solution)/shard_map/tile_parts/pallas_call | solution.py:298
  8.8 0.0 collective-permute-done.earlier_ref
  8.8 0.0 copy-start.1
  8.8 0.6 copy-done.1
  9.3 2.3 %fine_resid.1 = (f32[8,64]{1,0:T(8,128)}, f32[392,128]{1,0:T(8,128)}) custom-call(bf16[512,512]{1,0:T(8,128)(2,1)} %bitcast.9, f32[8,64]{1,0:T(8,128)} %resid_ref.3, bf16[8,64]{1,0:T(8,128)(2,1)} %get-tuple-element.21.rounded_ref, bf16[8,64]{1,0:T(8,128)(2,1)} %copy-done.1, s32[8,8,128]{2,1,0:T(8,128)} %get-tuple-element.19.cols_ref, ...), custom_call_target="tpu_custom_call" | custom-call | tf_op jit(solution)/shard_map/fine_resid/pallas_call | solution.py:298
  11.7 2.0 %collective-permute-start.1 = (f32[392,128]{1,0:T(8,128)}, f32[392,128]{1,0:T(8,128)S(1)}, u32[]{:S(2)}, u32[]{:S(2)}) collective-permute-start(f32[392,128]{1,0:T(8,128)} %get-tuple-element.22.sent_ref), channel_id=1, source_target_pairs={{0,2},{2,0},{4,6},{6,4},{8,10},{10,8},{12,14},{14,12},{16,18},{18,... | collective-permute-start | bytes 602120 | tf_op jit(solution)/shard_map/ppermute | solution.py:333
  13.7 6.4 %collective-permute-done.1.got_ref = f32[392,128]{1,0:T(8,128)S(1)} collective-permute-done((f32[392,128]{1,0:T(8,128)}, f32[392,128]{1,0:T(8,128)S(1)}, u32[]{:S(2)}, u32[]{:S(2)}) %collective-permute-start.1) | collective-permute-done | bytes 200736 | tf_op jit(solution)/shard_map/ppermute | solution.py:333
  20.1 0.0 copy-start
  20.1 0.7 copy-done
  20.8 4.5 %level_0.1 = (f32[8,64]{1,0:T(8,128)}, f32[8,64]{1,0:T(8,128)}, f32[800,128]{1,0:T(8,128)}) custom-call(bf16[512,512]{1,0:T(8,128)(2,1)} %bitcast.10, s32[8,8,128]{2,1,0:T(8,128)} %get-tuple-element.19.cols_ref, f32[4,4,64,128]{3,2,1,0:T(8,128)} %get-tuple-element.20.tiles_ref, f32[392,128]{1,0:T(8,128)} %get-tuple-element.22.sent_ref, f32[392,128]{1,0:T(8,128)} %copy-done, ...), custom_call_target="tpu_custom_call" | custom-call | tf_op jit(solution)/shard_map/level_0/pallas_call | solution.py:298
  25.2 15.3 %all_to_all.33 = f32[4,200,128]{2,1,0:T(8,128)} all-to-all(f32[4,200,128]{2,1,0:T(8,128)} %bitcast.17), channel_id=1, replica_groups={{0,2,4,6},{8,10,12,14},{16,18,20,22},{24,26,28,30},{1,3,5,7},{9,11,13,1..., dimensions={0} | all-to-all | bytes 819200 | tf_op jit(solution)/shard_map/all_to_all | solution.py:311
  40.5 4.5 %level_1.1 = (f32[8,64]{1,0:T(8,128)}, f32[8,64]{1,0:T(8,128)}, f32[832,128]{1,0:T(8,128)}) custom-call(bf16[512,512]{1,0:T(8,128)(2,1)} %bitcast.11, s32[8,8,128]{2,1,0:T(8,128)} %get-tuple-element.19.cols_ref, f32[4,4,64,128]{3,2,1,0:T(8,128)} %get-tuple-element.20.tiles_ref, f32[800,128]{1,0:T(8,128)} %bitcast.14, f32[8,64]{1,0:T(8,128)} %get-tuple-element.26.fresid_ref, ...), custom_call_target="tpu_custom_call" | custom-call | tf_op jit(solution)/shard_map/level_1/pallas_call | solution.py:298
  45.0 33.1 %all_to_all.34 = f32[8,104,128]{2,1,0:T(8,128)} all-to-all(f32[8,104,128]{2,1,0:T(8,128)} %bitcast.16), channel_id=1, replica_groups={{0,2,4,6,8,10,12,14},{16,18,20,22,24,26,28,30},{1,3,5,7,9,11,13,15},{17..., dimensions={0} | all-to-all | bytes 851968 | tf_op jit(solution)/shard_map/all_to_all | solution.py:311
  78.1 4.3 %level_2.1 = (f32[8,64]{1,0:T(8,128)}, f32[640,128]{1,0:T(8,128)}) custom-call(bf16[512,512]{1,0:T(8,128)(2,1)} %bitcast.12, s32[8,8,128]{2,1,0:T(8,128)} %get-tuple-element.19.cols_ref, f32[832,128]{1,0:T(8,128)} %bitcast.13, f32[8,64]{1,0:T(8,128)} %get-tuple-element.29.fresid_ref, f32[8,64]{1,0:T(8,128)} %get-tuple-element.30.total_ref), custom_call_target="tpu_custom_call" | custom-call | tf_op jit(solution)/shard_map/level_2/pallas_call | solution.py:298
  82.3 55.9 %all_to_all.35 = f32[16,40,128]{2,1,0:T(8,128)} all-to-all(f32[16,40,128]{2,1,0:T(8,128)} %bitcast.18), channel_id=1, replica_groups={{0,2,4,6,8,10,12,14,16,18,20,22,24,26,28,30},{1,3,5,7,9,11,13,15,17,19,..., dimensions={0} | all-to-all | bytes 655360 | tf_op jit(solution)/shard_map/all_to_all | solution.py:311
  138.2 3.5 %level_3.1 = f32[8,64]{1,0:T(8,128)} custom-call(s32[8,8,128]{2,1,0:T(8,128)} %get-tuple-element.19.cols_ref, f32[640,128]{1,0:T(8,128)} %bitcast.15, f32[8,64]{1,0:T(8,128)} %get-tuple-element.32.total_ref), custom_call_target="tpu_custom_call" | custom-call | tf_op jit(solution)/shard_map/level_3/pallas_call | solution.py:298
Async XLA Ops:
  3.6 1.9 %copy-start.2 = (s32[1,3,8]{2,0,1:T(1,128)S(1)}, s32[1,3,8]{2,0,1:T(1,128)}, u32[]{:S(2)}) copy-start(s32[1,3,8]{2,0,1:T(1,128)} %param.9) | copy-start | bytes 292
  3.6 5.1 %collective-permute-start = (bf16[8,64]{1,0:T(8,128)(2,1)}, bf16[8,64]{1,0:T(8,128)(2,1)S(1)}, u32[]{:S(2)}, u32[]{:S(2)}) collective-permute-start(bf16[8,64]{1,0:T(8,128)(2,1)} %get-tuple-element.21.rounded_ref), channel_id=1, source_target_pairs={{0,1},{2,3},{4,5},{6,7},{8,9},{10,11},{12,13},{14,15},{16,17},{18,... | collective-permute-start | bytes 3080 | tf_op jit(solution)/shard_map/ppermute | solution.py:318
  8.8 0.6 copy-start.1
  11.7 8.4 %collective-permute-start.1 = (f32[392,128]{1,0:T(8,128)}, f32[392,128]{1,0:T(8,128)S(1)}, u32[]{:S(2)}, u32[]{:S(2)}) collective-permute-start(f32[392,128]{1,0:T(8,128)} %get-tuple-element.22.sent_ref), channel_id=1, source_target_pairs={{0,2},{2,0},{4,6},{6,4},{8,10},{10,8},{12,14},{14,12},{16,18},{18,... | collective-permute-start | bytes 602120 | tf_op jit(solution)/shard_map/ppermute | solution.py:333
  20.1 0.7 copy-start

commit v2 on v1

--- a/solution.py
+++ b/solution.py
@@ -14,6 +14,7 @@
 PAIRS = COARSE // 2
 WIDE = 2 * BLOCK
 ROWS = COARSE
+GRANT = 12 * 2**20
 INTERPRET = False
 
 F32 = jnp.float32
@@ -103,14 +104,12 @@
     for q in range(PAIRS):
         along = jnp.sum(jnp.where(own_lanes(q), inverse, 0.0), axis=0, keepdims=True)
         first.append(one - pairs[q] * along)
+    y = values + applied(operand(first), values)
     second = [squared(e) for e in first]
-    fourth = [squared(e) for e in second]
-    w1, w2, w4 = operand(first), operand(second), operand(fourth)
-    y = values
-    y = y + applied(w4, applied(w4, y))
-    y = y + applied(w4, y)
-    y = y + applied(w2, y)
-    y = y + applied(w1, y)
+    y = y + applied(operand(second), y)
+    fourth = operand([squared(e) for e in second])
+    y = y + applied(fourth, y)
+    y = y + applied(fourth, applied(fourth, y))
     return y * inverse
 
 
@@ -156,7 +155,7 @@
     def label(j, level):
         value = fine_map_ref[j]
         for step in range(level):
-            value = maps_ref[0, step, value]
+            value = maps_ref[step, 0, value]
         return value
 
     index = [jnp.where(first_half, rows, -1)] + [jnp.full((ROWS, WIDE), -1, I32) for q in range(PAIRS - 1)]
@@ -193,17 +192,43 @@
             tiles_ref[level, q] = jnp.where(wide_left, even, odd) + moved
 
 
-def store_rows(out_ref, start, values):
-    out_ref[start : start + ROWS, :] = twice(values)
-
-
-SEND0 = ROWS + PAIRS * BLOCK + 2 * BLOCK
-SEND1 = ROWS + 2 * BLOCK + BLOCK
-SEND2 = ROWS + BLOCK + BLOCK // 2
-SEND3 = ROWS + BLOCK // 2
-
-
-def resid_kernel(ops_ref, resid_ref, rounded_ref, earlier_ref, cols_ref, tiles_ref, fresid_ref, send_ref):
+HEAD = 2 * ROWS
+HALF = BLOCK // 2
+SEND0 = HEAD + 2 * PAIRS * BLOCK + 2 * BLOCK
+SEND1 = HEAD + 2 * BLOCK + BLOCK
+SEND2 = HEAD + BLOCK + HALF
+SEND3 = HEAD + HALF
+
+
+def on_diagonal(size, start):
+    return iota((size, WIDE), 0) + start == iota((size, WIDE), 1) % BLOCK
+
+
+def packed(values, parts):
+    head = jnp.concatenate([values.astype(BF16).astype(F32), values - values.astype(BF16).astype(F32)], axis=1)
+    rows = iota((ROWS, WIDE), 0)
+    lows = jnp.zeros((ROWS, WIDE), F32)
+    body = []
+    for i, (part, start) in enumerate(parts):
+        high, low = split(part)
+        body.append(high)
+        along = jnp.where(on_diagonal(part.shape[0], start), low.astype(F32), 0.0)
+        lows = jnp.where(rows == i, jnp.sum(along, axis=0, keepdims=True), lows)
+    return jnp.concatenate([jnp.concatenate([head, lows], axis=0).astype(BF16)] + body, axis=0)
+
+
+def got_rows(ref, base):
+    head = ref[base : base + HEAD, :].astype(F32)[:ROWS]
+    return head[:, :BLOCK] + head[:, BLOCK:]
+
+
+def got_part(ref, base, i, at, size, start):
+    low = ref[base : base + HEAD, :].astype(F32)[ROWS + i : ROWS + i + 1]
+    high = ref[base + at : base + at + size, :].astype(F32)
+    return high + jnp.where(on_diagonal(size, start), low, 0.0)
+
+
+def resid_kernel(ops_ref, resid_ref, rounded_ref, earlier_ref, cols_ref, tiles_ref, fresid_ref, rows_ref, send_ref):
     own = twice(rounded_ref[...].astype(F32))
     before = twice(earlier_ref[...].astype(F32))
     tiles = gathered(cols_ref, own)
@@ -212,13 +237,16 @@
     stacked = jnp.concatenate([stacked, jnp.zeros_like(stacked)], axis=0).astype(BF16)
     fresid = resid_ref[...] - fold(product_nt(stacked, ops_ref[...])[:ROWS])
     fresid_ref[...] = fresid
-    store_rows(send_ref, 0, restricted(cols_ref[PAIRS][:, :BLOCK], fresid))
+    rows = restricted(cols_ref[PAIRS][:, :BLOCK], fresid)
+    rows_ref[...] = rows
     other = 1 - lax.rem(lax.axis_index("gy"), 2)
-    for q in range(PAIRS):
-        send_ref[ROWS + q * BLOCK : ROWS + (q + 1) * BLOCK, :] = tiles_ref[0, q]
-    at = ROWS + PAIRS * BLOCK
-    for i in range(2):
-        send_ref[at + i * BLOCK : at + (i + 1) * BLOCK, :] = tiles_ref[1, 2 * other + i]
+    send_ref[:HEAD + 2 * BLOCK, :] = packed(rows, [(tiles_ref[1, 2 * other + i], 0) for i in range(2)])
+    at = HEAD + 2 * BLOCK
+    for q in range(PAIRS):
+        high, low = split(tiles_ref[0, q])
+        send_ref[at : at + BLOCK, :] = high
+        send_ref[at + BLOCK : at + 2 * BLOCK, :] = low
+        at += 2 * BLOCK
 
 
 def descend(level, pairs, coarse_rows, ops_ref, cols_ref, fresid_ref, total_ref, fresid_out, total_out):
@@ -228,65 +256,60 @@
     fresid = fresid_ref[...] - ops_product(ops_ref, gathered(cols_ref, twice(on_fine)))
     if fresid_out is not None:
         fresid_out[...] = fresid
-    return twice(restricted(cols_ref[PAIRS + level + 1][:, :BLOCK], fresid))
-
-
-def level0_kernel(ops_ref, cols_ref, tiles_ref, sent_ref, got_ref, fresid_ref, total_ref, fresid_out, total_out, send_ref):
+    return restricted(cols_ref[PAIRS + level + 1][:, :BLOCK], fresid)
+
+
+def level0_kernel(ops_ref, cols_ref, tiles_ref, rows_ref, got_ref, fresid_ref, total_ref, fresid_out, total_out, send_ref):
     half = lax.rem(lax.axis_index("gy"), 2)
-    pairs = [
-        tiles_ref[0, q] + got_ref[ROWS + q * BLOCK : ROWS + (q + 1) * BLOCK, :] for q in range(PAIRS)
-    ]
-    coarse_rows = sent_ref[:ROWS, :BLOCK] + got_ref[:ROWS, :BLOCK]
-    at = ROWS + PAIRS * BLOCK
-    summed = [tiles_ref[1, 2 * half + i] + got_ref[at + i * BLOCK : at + (i + 1) * BLOCK, :] for i in range(2)]
+    at = HEAD + 2 * BLOCK
+    pairs = []
+    for q in range(PAIRS):
+        high = got_ref[at : at + BLOCK, :].astype(F32)
+        low = got_ref[at + BLOCK : at + 2 * BLOCK, :].astype(F32)
+        pairs.append(tiles_ref[0, q] + high + low)
+        at += 2 * BLOCK
+    coarse_rows = rows_ref[...] + got_rows(got_ref, 0)
+    summed = [tiles_ref[1, 2 * half + i] + got_part(got_ref, 0, i, HEAD + i * BLOCK, BLOCK, 0) for i in range(2)]
     rows = descend(0, pairs, coarse_rows, ops_ref, cols_ref, fresid_ref, total_ref, fresid_out, total_out)
     for e in range(4):
-        base = e * SEND1
-        send_ref[base : base + ROWS, :] = rows
-        for i in range(2):
-            send_ref[base + ROWS + i * BLOCK : base + ROWS + (i + 1) * BLOCK, :] = summed[i]
-        send_ref[base + ROWS + 2 * BLOCK : base + SEND1, :] = tiles_ref[2, e]
+        parts = [(summed[0], 0), (summed[1], 0), (tiles_ref[2, e], 0)]
+        send_ref[e * SEND1 : (e + 1) * SEND1, :] = packed(rows, parts)
 
 
 def level1_kernel(ops_ref, cols_ref, tiles_ref, got_ref, fresid_ref, total_ref, fresid_out, total_out, send_ref):
-    def chunk(e, start, size):
-        return got_ref[e * SEND1 + start : e * SEND1 + start + size, :]
-
-    coarse_rows = sum(chunk(e, 0, ROWS) for e in range(4))[:, :BLOCK]
+    coarse_rows = sum(got_rows(got_ref, e * SEND1) for e in range(4))
     pairs = []
     for q in range(PAIRS):
         half, i = q // 2, q % 2
-        pairs.append(chunk(half, ROWS + i * BLOCK, BLOCK) + chunk(half + 2, ROWS + i * BLOCK, BLOCK))
-    summed = sum(chunk(e, ROWS + 2 * BLOCK, BLOCK) for e in range(4))
+        pairs.append(
+            sum(got_part(got_ref, e * SEND1, i, HEAD + i * BLOCK, BLOCK, 0) for e in (half, half + 2))
+        )
+    summed = sum(got_part(got_ref, e * SEND1, 2, HEAD + 2 * BLOCK, BLOCK, 0) for e in range(4))
     rows = descend(1, pairs, coarse_rows, ops_ref, cols_ref, fresid_ref, total_ref, fresid_out, total_out)
     for e in range(8):
-        base = e * SEND2
-        send_ref[base : base + ROWS, :] = rows
-        send_ref[base + ROWS : base + ROWS + BLOCK, :] = summed
-        part = BLOCK // 2 * (e % 2)
-        send_ref[base + ROWS + BLOCK : base + SEND2, :] = tiles_ref[3, e // 2, part : part + BLOCK // 2, :]
+        start = HALF * (e % 2)
+        parts = [(summed, 0), (tiles_ref[3, e // 2, start : start + HALF, :], start)]
+        send_ref[e * SEND2 : (e + 1) * SEND2, :] = packed(rows, parts)
 
 
 def level2_kernel(ops_ref, cols_ref, got_ref, fresid_ref, total_ref, total_out, send_ref):
-    def chunk(e, start, size):
-        return got_ref[e * SEND2 + start : e * SEND2 + start + size, :]
-
-    coarse_rows = sum(chunk(e, 0, ROWS) for e in range(8))[:, :BLOCK]
-    pairs = [chunk(q, ROWS, BLOCK) + chunk(q + 4, ROWS, BLOCK) for q in range(PAIRS)]
-    summed = sum(chunk(e, ROWS + BLOCK, BLOCK // 2) for e in range(8))
+    coarse_rows = sum(got_rows(got_ref, e * SEND2) for e in range(8))
+    pairs = [
+        sum(got_part(got_ref, e * SEND2, 0, HEAD, BLOCK, 0) for e in (q, q + 4)) for q in range(PAIRS)
+    ]
+    start = HALF * lax.rem(lax.axis_index("gy"), 2)
+    summed = sum(got_part(got_ref, e * SEND2, 1, HEAD + BLOCK, HALF, start) for e in range(8))
     rows = descend(2, pairs, coarse_rows, ops_ref, cols_ref, fresid_ref, total_ref, None, total_out)
+    chunk = packed(rows, [(summed, start)])
     for e in range(16):
-        base = e * SEND3
-        send_ref[base : base + ROWS, :] = rows
-        send_ref[base + ROWS : base + SEND3, :] = summed
+        send_ref[e * SEND3 : (e + 1) * SEND3, :] = chunk
 
 
 def level3_kernel(cols_ref, got_ref, total_ref, out_ref):
-    def chunk(e, start, size):
-        return got_ref[e * SEND3 + start : e * SEND3 + start + size, :]
-
-    coarse_rows = sum(chunk(e, 0, ROWS) for e in range(16))[:, :BLOCK]
-    eighths = [chunk(e, ROWS, BLOCK // 2) + chunk(e + 8, ROWS, BLOCK // 2) for e in range(8)]
+    coarse_rows = sum(got_rows(got_ref, e * SEND3) for e in range(16))
+    eighths = [
+        sum(got_part(got_ref, e * SEND3, 0, HEAD, HALF, HALF * (p % 2)) for e in (p, p + 8)) for p in range(8)
+    ]
     pairs = [jnp.concatenate([eighths[2 * q], eighths[2 * q + 1]], axis=0) for q in range(PAIRS)]
     out = smooth(pairs, coarse_rows)
     out_ref[...] = total_ref[...] + picked(cols_ref[PAIRS + 3][:, :BLOCK], out)
@@ -302,6 +325,7 @@
         in_specs=[smem] * scalars + [vmem] * (len(args) - scalars),
         out_specs=[vmem] * len(out_shapes),
         scratch_shapes=list(scratch),
+        compiler_params=pltpu.CompilerParams(vmem_limit_bytes=GRANT),
         interpret=INTERPRET,
     )(*args)
 
@@ -320,35 +344,35 @@
         tiles_kernel,
         "tile_parts",
         [((PAIRS + LEVELS, ROWS, WIDE), I32), ((LEVELS, PAIRS, BLOCK, WIDE), F32)],
-        [neighbours, fine_map, coarse_maps, ops],
+        [neighbours, fine_map, jnp.transpose(coarse_maps, (1, 0, 2)), ops],
         scalars=3,
         scratch=[pltpu.VMEM((LEVELS, COARSE, BLOCK, WIDE), F32)],
     )
-    fresid, sent = call(
+    fresid, rows, sent = call(
         resid_kernel,
         "fine_resid",
-        [(vec, F32), ((SEND0, WIDE), F32)],
+        [(vec, F32), (vec, F32), ((SEND0, WIDE), BF16)],
         [ops, residual, rounded, earlier, cols, tiles],
     )
     got = lax.ppermute(sent, "gy", [(i, i ^ 1) for i in range(lax.axis_size("gy"))])
     fresid, total, chunks = call(
         level0_kernel,
         "level_0",
-        [(vec, F32), (vec, F32), ((4 * SEND1, WIDE), F32)],
-        [ops, cols, tiles, sent, got, fresid, fine_smooth],
+        [(vec, F32), (vec, F32), ((4 * SEND1, WIDE), BF16)],
+        [ops, cols, tiles, rows, got, fresid, fine_smooth],
     )
     got = shared(chunks, 4)
     fresid, total, chunks = call(
         level1_kernel,
         "level_1",
-        [(vec, F32), (vec, F32), ((8 * SEND2, WIDE), F32)],
+        [(vec, F32), (vec, F32), ((8 * SEND2, WIDE), BF16)],
         [ops, cols, tiles, got, fresid, total],
     )
     got = shared(chunks, 8)
     total, chunks = call(
         level2_kernel,
         "level_2",
-        [(vec, F32), ((16 * SEND3, WIDE), F32)],
+        [(vec, F32), ((16 * SEND3, WIDE), BF16)],
         [ops, cols, got, fresid, total],
     )
     got = shared(chunks, 16)

time: 142 us -> 102 us (0.72)
  the two profiles are of different devices: /device:TPU:60 before, /device:TPU:58 now
where the time goes in v2:
time: 102 us; the launch traced here: 101 us
  blocking collectives  78.4 us (77%)
  Pallas kernels  11.7 us (11%)
  waiting for transfers between devices  5.69 us (6%)
  starting transfers between devices  3.9 us (4%)
  local copies, waits for them, and re-layouts  1.74 us (2%)
    all_to_all x3, blocking collectives, shared(): lax.all_to_all(chunks, 'gy', 0, 0, axis_index_groups=lists, tiled=True)  78.4 us
    pallas_call x7, Pallas kernels, call(): pl.pallas_call(kernel, name=name, out_shape=[jax.ShapeDtypeStruct(shape,...  11.7 us
    ppermute x1, waiting for transfers between devices, on_device(): lax.ppermute(sent, 'gy', [(i, i ^ 1) for i in range(lax.axis_size('gy'))])  5.69 us
  transfers between devices with their start and end apart: 2, of which 1 were waited for; matrix products, arithmetic and copies ran while one was open for 0% of the time, Pallas kernels for 1%

profile of v2, /device:TPU:58, one launch (start us, length us, event | category | flops | bytes accessed | tf_op | source)
XLA Modules:
  0.0 101.5 jit_solution(4652733352177993406)
XLA Ops:
  0.0 0.0 copy-start
  0.0 1.0 %copy-done = bf16[8,64,512]{2,1,0:T(8,128)(2,1)S(1)} copy-done((bf16[8,64,512]{2,1,0:T(8,128)(2,1)S(1)}, bf16[8,64,512]{2,1,0:T(8,128)(2,1)}, u32[]{:S(2)}) %copy-start) | copy-done | bytes 524312
  1.0 0.0 copy-start.2
  1.0 0.7 copy-done.2
  1.7 0.0 copy-start.1
  1.7 0.0 copy-start.3
  1.7 1.6 %fine_smooth.1 = (f32[8,64]{1,0:T(8,128)S(1)}, bf16[8,64]{1,0:T(8,128)(2,1)S(1)}) custom-call(bf16[512,512]{1,0:T(8,128)(2,1)S(1)} %bitcast.8, f32[8,64]{1,0:T(8,128)S(1)} %copy-done.2), custom_call_target="tpu_custom_call" | custom-call | tf_op jit(solution)/shard_map/fine_smooth/pallas_call | solution.py:321
  3.3 0.0 copy-start.4
  3.3 0.0 copy-start.5
  3.3 1.9 %collective-permute-start = (bf16[8,64]{1,0:T(8,128)(2,1)S(1)}, bf16[8,64]{1,0:T(8,128)(2,1)S(1)}, u32[]{:S(2)}, u32[]{:S(2)}) collective-permute-start(bf16[8,64]{1,0:T(8,128)(2,1)S(1)} %get-tuple-element.22.rounded_ref), channel_id=1, source_target_pairs={{0,1},{2,3},{4,5},{6,7},{8,9},{10,11},{12,13},{14,15},{16,17},{18,... | collective-permute-start | bytes 3080 | tf_op jit(solution)/shard_map/ppermute | solution.py:342
  5.2 0.0 copy-done.1
  5.2 0.0 copy-done.3
  5.2 0.0 copy-done.4
  5.2 0.0 copy-done.5
  5.3 1.5 %tile_parts.1 = (s32[8,8,128]{2,1,0:T(8,128)S(1)}, f32[4,4,64,128]{3,2,1,0:T(8,128)S(1)}) custom-call(s32[8,6]{1,0:T(8,128)S(1)} %copy-done.3, s32[8]{0:T(128)S(1)} %copy-done.5, s32[3,1,8]{2,1,0:T(1,128)S(1)} %bitcast.20, bf16[512,512]{1,0:T(8,128)(2,1)S(1)} %bitcast.9), custom_call_target="tpu_custom_call" | custom-call | tf_op jit(solution)/shard_map/tile_parts/pallas_call | solution.py:321
  6.7 0.0 collective-permute-done.earlier_ref
  6.7 0.4 fine_resid.1
  7.2 2.0 %collective-permute-start.1 = (bf16[656,128]{1,0:T(8,128)(2,1)S(1)}, bf16[656,128]{1,0:T(8,128)(2,1)S(1)}, u32[]{:S(2)}, u32[]{:S(2)}) collective-permute-start(bf16[656,128]{1,0:T(8,128)(2,1)S(1)} %get-tuple-element.24), channel_id=1, source_target_pairs={{0,2},{2,0},{4,6},{6,4},{8,10},{10,8},{12,14},{14,12},{16,18},{18,... | collective-permute-start | bytes 503816 | tf_op jit(solution)/shard_map/ppermute | solution.py:357
  9.2 5.7 %collective-permute-done.1.got_ref = bf16[656,128]{1,0:T(8,128)(2,1)S(1)} collective-permute-done((bf16[656,128]{1,0:T(8,128)(2,1)S(1)}, bf16[656,128]{1,0:T(8,128)(2,1)S(1)}, u32[]{:S(2)}, u32[]{:S(2)}) %collective-permute-start.1) | collective-permute-done | bytes 167968 | tf_op jit(solution)/shard_map/ppermute | solution.py:357
  14.9 2.0 %level_0.1 = (f32[8,64]{1,0:T(8,128)S(1)}, f32[8,64]{1,0:T(8,128)S(1)}, bf16[832,128]{1,0:T(8,128)(2,1)S(1)}) custom-call(bf16[512,512]{1,0:T(8,128)(2,1)S(1)} %bitcast.11, s32[8,8,128]{2,1,0:T(8,128)S(1)} %get-tuple-element.20.cols_ref, f32[4,4,64,128]{3,2,1,0:T(8,128)S(1)} %get-tuple-element.21.tiles_ref, f32[8,64]{1,0:T(8,128)S(1)} %get-tuple-element.23.rows_ref, ...), custom_call_target="tpu_custom_call" | custom-call | tf_op jit(solution)/shard_map/level_0/pallas_call | solution.py:321
  16.9 11.6 %all_to_all.33 = bf16[4,208,128]{2,1,0:T(8,128)(2,1)S(1)} all-to-all(bf16[4,208,128]{2,1,0:T(8,128)(2,1)S(1)} %bitcast.18), channel_id=1, replica_groups={{0,2,4,6},{8,10,12,14},{16,18,20,22},{24,26,28,30},{1,3,5,7},{9,11,13,1..., dimensions={0} | all-to-all | bytes 425984 | tf_op jit(solution)/shard_map/all_to_all | solution.py:335
  28.5 2.0 %level_1.1 = (f32[8,64]{1,0:T(8,128)S(1)}, f32[8,64]{1,0:T(8,128)S(1)}, bf16[896,128]{1,0:T(8,128)(2,1)S(1)}) custom-call(bf16[512,512]{1,0:T(8,128)(2,1)S(1)} %bitcast.12, s32[8,8,128]{2,1,0:T(8,128)S(1)} %get-tuple-element.20.cols_ref, f32[4,4,64,128]{3,2,1,0:T(8,128)S(1)} %get-tuple-element.21.tiles_ref, bf16[832,128]{1,0:T(8,128)(2,1)S(1)} %bitcast.15, ...), custom_call_target="tpu_custom_call" | custom-call | tf_op jit(solution)/shard_map/level_1/pallas_call | solution.py:321
  30.5 23.0 %all_to_all.34 = bf16[8,112,128]{2,1,0:T(8,128)(2,1)S(1)} all-to-all(bf16[8,112,128]{2,1,0:T(8,128)(2,1)S(1)} %bitcast.17), channel_id=1, replica_groups={{0,2,4,6,8,10,12,14},{16,18,20,22,24,26,28,30},{1,3,5,7,9,11,13,15},{17..., dimensions={0} | all-to-all | bytes 458752 | tf_op jit(solution)/shard_map/all_to_all | solution.py:335
  53.5 2.0 %level_2.1 = (f32[8,64]{1,0:T(8,128)S(1)}, bf16[768,128]{1,0:T(8,128)(2,1)S(1)}) custom-call(bf16[512,512]{1,0:T(8,128)(2,1)S(1)} %bitcast.13, s32[8,8,128]{2,1,0:T(8,128)S(1)} %get-tuple-element.20.cols_ref, bf16[896,128]{1,0:T(8,128)(2,1)S(1)} %bitcast.14, f32[8,64]{1,0:T(8,128)S(1)} %get-tuple-element.31.fresid_ref, f32[8,64]{1,0:T(8,128)S(1)} %get-tuple-element.32.total_ref), custom_call_target="tpu_custom_call" | custom-call | tf_op jit(solution)/shard_map/level_2/pallas_call | solution.py:321
  55.5 43.8 %all_to_all.35 = bf16[16,48,128]{2,1,0:T(8,128)(2,1)S(1)} all-to-all(bf16[16,48,128]{2,1,0:T(8,128)(2,1)S(1)} %bitcast.19), channel_id=1, replica_groups={{0,2,4,6,8,10,12,14,16,18,20,22,24,26,28,30},{1,3,5,7,9,11,13,15,17,19,..., dimensions={0} | all-to-all | bytes 393216 | tf_op jit(solution)/shard_map/all_to_all | solution.py:335
  99.3 2.2 %level_3.1 = f32[8,64]{1,0:T(8,128)} custom-call(s32[8,8,128]{2,1,0:T(8,128)S(1)} %get-tuple-element.20.cols_ref, bf16[768,128]{1,0:T(8,128)(2,1)S(1)} %bitcast.16, f32[8,64]{1,0:T(8,128)S(1)} %get-tuple-element.34.total_ref), custom_call_target="tpu_custom_call" | custom-call | tf_op jit(solution)/shard_map/level_3/pallas_call | solution.py:321
Async XLA Ops:
  0.0 1.0 %copy-start = (bf16[8,64,512]{2,1,0:T(8,128)(2,1)S(1)}, bf16[8,64,512]{2,1,0:T(8,128)(2,1)}, u32[]{:S(2)}) copy-start(bf16[8,64,512]{2,1,0:T(8,128)(2,1)} %param.6) | copy-start | bytes 1572868
  1.0 0.7 copy-start.2
  1.7 3.5 %copy-start.1 = (bf16[8,64,512]{2,1,0:T(8,128)(2,1)S(1)}, bf16[8,64,512]{2,1,0:T(8,128)(2,1)}, u32[]{:S(2)}) copy-start(bf16[8,64,512]{2,1,0:T(8,128)(2,1)} %param.6) | copy-start | bytes 1572868
  1.7 3.5 %copy-start.3 = (s32[8,6]{1,0:T(8,128)S(1)}, s32[8,6]{1,0:T(8,128)}, u32[]{:S(2)}) copy-start(s32[8,6]{1,0:T(8,128)} %near_ref.1) | copy-start | bytes 580
  3.3 1.9 %copy-start.4 = (s32[1,3,8]{2,0,1:T(1,128)S(1)}, s32[1,3,8]{2,0,1:T(1,128)}, u32[]{:S(2)}) copy-start(s32[1,3,8]{2,0,1:T(1,128)} %param.9) | copy-start | bytes 292
  3.3 1.9 %copy-start.5 = (s32[8]{0:T(128)S(1)}, s32[8]{0:T(128)}, u32[]{:S(2)}) copy-start(s32[8]{0:T(128)} %fine_map_ref.1) | copy-start | bytes 100
  3.3 3.4 %collective-permute-start = (bf16[8,64]{1,0:T(8,128)(2,1)S(1)}, bf16[8,64]{1,0:T(8,128)(2,1)S(1)}, u32[]{:S(2)}, u32[]{:S(2)}) collective-permute-start(bf16[8,64]{1,0:T(8,128)(2,1)S(1)} %get-tuple-element.22.rounded_ref), channel_id=1, source_target_pairs={{0,1},{2,3},{4,5},{6,7},{8,9},{10,11},{12,13},{14,15},{16,17},{18,... | collective-permute-start | bytes 3080 | tf_op jit(solution)/shard_map/ppermute | solution.py:342
  7.2 7.7 %collective-permute-start.1 = (bf16[656,128]{1,0:T(8,128)(2,1)S(1)}, bf16[656,128]{1,0:T(8,128)(2,1)S(1)}, u32[]{:S(2)}, u32[]{:S(2)}) collective-permute-start(bf16[656,128]{1,0:T(8,128)(2,1)S(1)} %get-tuple-element.24), channel_id=1, source_target_pairs={{0,2},{2,0},{4,6},{6,4},{8,10},{10,8},{12,14},{14,12},{16,18},{18,... | collective-permute-start | bytes 503816 | tf_op jit(solution)/shard_map/ppermute | solution.py:357

commit v3 on v2

--- a/solution.py
+++ b/solution.py
@@ -292,7 +292,7 @@
         send_ref[e * SEND2 : (e + 1) * SEND2, :] = packed(rows, parts)
 
 
-def level2_kernel(ops_ref, cols_ref, got_ref, fresid_ref, total_ref, total_out, send_ref):
+def level2_kernel(ops_ref, cols_ref, got_ref, fresid_ref, total_ref, total_out, rows_out, part_out, send_ref):
     coarse_rows = sum(got_rows(got_ref, e * SEND2) for e in range(8))
     pairs = [
         sum(got_part(got_ref, e * SEND2, 0, HEAD, BLOCK, 0) for e in (q, q + 4)) for q in range(PAIRS)
@@ -300,16 +300,22 @@
     start = HALF * lax.rem(lax.axis_index("gy"), 2)
     summed = sum(got_part(got_ref, e * SEND2, 1, HEAD + BLOCK, HALF, start) for e in range(8))
     rows = descend(2, pairs, coarse_rows, ops_ref, cols_ref, fresid_ref, total_ref, None, total_out)
-    chunk = packed(rows, [(summed, start)])
-    for e in range(16):
+    rows_out[...] = rows
+    part_out[...] = summed
+    send_ref[...] = packed(rows, [(summed, start)])
+
+
+def join_kernel(rows_ref, part_ref, got_ref, send_ref):
+    start = HALF * lax.rem(lax.axis_index("gy"), 2)
+    rows = rows_ref[...] + got_rows(got_ref, 0)
+    chunk = packed(rows, [(part_ref[...] + got_part(got_ref, 0, 0, HEAD, HALF, start), start)])
+    for e in range(8):
         send_ref[e * SEND3 : (e + 1) * SEND3, :] = chunk
 
 
 def level3_kernel(cols_ref, got_ref, total_ref, out_ref):
-    coarse_rows = sum(got_rows(got_ref, e * SEND3) for e in range(16))
-    eighths = [
-        sum(got_part(got_ref, e * SEND3, 0, HEAD, HALF, HALF * (p % 2)) for e in (p, p + 8)) for p in range(8)
-    ]
+    coarse_rows = sum(got_rows(got_ref, e * SEND3) for e in range(8))
+    eighths = [got_part(got_ref, e * SEND3, 0, HEAD, HALF, HALF * (e % 2)) for e in range(8)]
     pairs = [jnp.concatenate([eighths[2 * q], eighths[2 * q + 1]], axis=0) for q in range(PAIRS)]
     out = smooth(pairs, coarse_rows)
     out_ref[...] = total_ref[...] + picked(cols_ref[PAIRS + 3][:, :BLOCK], out)
@@ -335,6 +341,10 @@
     return lax.all_to_all(chunks, "gy", 0, 0, axis_index_groups=lists, tiled=True)
 
 
+def crossed(value, distance):
+    return lax.ppermute(value, "gy", [(i, i ^ distance) for i in range(lax.axis_size("gy"))])
+
+
 def on_device(residual, fine_ops, neighbours, fine_map, coarse_maps):
     ops = fine_ops.reshape(FINE_BLOCKS * BLOCK, SLOTS * BLOCK)
     vec = (FINE_BLOCKS, BLOCK)
@@ -354,7 +364,7 @@
         [(vec, F32), (vec, F32), ((SEND0, WIDE), BF16)],
         [ops, residual, rounded, earlier, cols, tiles],
     )
-    got = lax.ppermute(sent, "gy", [(i, i ^ 1) for i in range(lax.axis_size("gy"))])
+    got = crossed(sent, 1)
     fresid, total, chunks = call(
         level0_kernel,
         "level_0",
@@ -369,13 +379,15 @@
         [ops, cols, tiles, got, fresid, total],
     )
     got = shared(chunks, 8)
-    total, chunks = call(
+    total, rows, part, sent = call(
         level2_kernel,
         "level_2",
-        [(vec, F32), ((16 * SEND3, WIDE), BF16)],
+        [(vec, F32), (vec, F32), ((HALF, WIDE), F32), ((SEND3, WIDE), BF16)],
         [ops, cols, got, fresid, total],
     )
-    got = shared(chunks, 16)
+    got = crossed(sent, 8)
+    (chunks,) = call(join_kernel, "join", [((8 * SEND3, WIDE), BF16)], [rows, part, got])
+    got = shared(chunks, 8)
     (out,) = call(level3_kernel, "level_3", [(vec, F32)], [cols, got, total])
     return out
 

time: 102 us -> 91.9 us (0.901)
  the two profiles are of different devices: /device:TPU:58 before, /device:TPU:26 now
where the time goes in v3:
time: 91.9 us; the launch traced here: 91.5 us
  blocking collectives  50.7 us (55%)
  starting transfers between devices  21.4 us (23%)
  Pallas kernels  11.8 us (13%)
  waiting for transfers between devices  5.72 us (6%)
  local copies, waits for them, and re-layouts  1.74 us (2%)
    all_to_all x3, blocking collectives, shared(): lax.all_to_all(chunks, 'gy', 0, 0, axis_index_groups=lists, tiled=True)  50.7 us
    ppermute x2, starting transfers between devices, crossed(): lax.ppermute(value, 'gy', [(i, i ^ distance) for i in range(lax.axis_size...  19.6 us
    pallas_call x8, Pallas kernels, call(): pl.pallas_call(kernel, name=name, out_shape=[jax.ShapeDtypeStruct(shape,...  11.8 us
    ppermute x2, waiting for transfers between devices, crossed(): lax.ppermute(value, 'gy', [(i, i ^ distance) for i in range(lax.axis_size...  5.72 us
    ppermute x1, starting transfers between devices, on_device(): earlier = lax.ppermute(rounded, 'ta', [(0, 1)])  1.89 us
  transfers between devices with their start and end apart: 3, of which 2 were waited for; matrix products, arithmetic and copies ran while one was open for 0% of the time, Pallas kernels for 2%

profile of v3, /device:TPU:26, one launch (start us, length us, event | category | flops | bytes accessed | tf_op | source)
XLA Modules:
  0.0 91.5 jit_solution(3873974575292291668)
XLA Ops:
  0.0 0.0 copy-start
  0.0 1.0 %copy-done = bf16[8,64,512]{2,1,0:T(8,128)(2,1)S(1)} copy-done((bf16[8,64,512]{2,1,0:T(8,128)(2,1)S(1)}, bf16[8,64,512]{2,1,0:T(8,128)(2,1)}, u32[]{:S(2)}) %copy-start) | copy-done | bytes 524312
  1.0 0.0 copy-start.2
  1.0 0.7 copy-done.2
  1.7 0.0 copy-start.1
  1.7 0.0 copy-start.3
  1.7 1.6 %fine_smooth.1 = (f32[8,64]{1,0:T(8,128)S(1)}, bf16[8,64]{1,0:T(8,128)(2,1)S(1)}) custom-call(bf16[512,512]{1,0:T(8,128)(2,1)S(1)} %bitcast.8, f32[8,64]{1,0:T(8,128)S(1)} %copy-done.2), custom_call_target="tpu_custom_call" | custom-call | tf_op jit(solution)/shard_map/fine_smooth/pallas_call | solution.py:327
  3.3 0.0 copy-start.4
  3.3 0.0 copy-start.5
  3.3 1.9 %collective-permute-start = (bf16[8,64]{1,0:T(8,128)(2,1)S(1)}, bf16[8,64]{1,0:T(8,128)(2,1)S(1)}, u32[]{:S(2)}, u32[]{:S(2)}) collective-permute-start(bf16[8,64]{1,0:T(8,128)(2,1)S(1)} %get-tuple-element.24.rounded_ref), channel_id=1, source_target_pairs={{0,1},{2,3},{4,5},{6,7},{8,9},{10,11},{12,13},{14,15},{16,17},{18,... | collective-permute-start | bytes 3080 | tf_op jit(solution)/shard_map/ppermute | solution.py:352
  5.2 0.0 copy-done.1
  5.2 0.0 copy-done.3
  5.2 0.0 copy-done.4
  5.2 0.0 copy-done.5
  5.2 1.5 %tile_parts.1 = (s32[8,8,128]{2,1,0:T(8,128)S(1)}, f32[4,4,64,128]{3,2,1,0:T(8,128)S(1)}) custom-call(s32[8,6]{1,0:T(8,128)S(1)} %copy-done.3, s32[8]{0:T(128)S(1)} %copy-done.5, s32[3,1,8]{2,1,0:T(1,128)S(1)} %bitcast.20, bf16[512,512]{1,0:T(8,128)(2,1)S(1)} %bitcast.9), custom_call_target="tpu_custom_call" | custom-call | tf_op jit(solution)/shard_map/tile_parts/pallas_call | solution.py:327
  6.7 0.0 collective-permute-done.earlier_ref
  6.7 0.4 fine_resid.1
  7.2 3.8 %collective-permute-start.1 = (bf16[656,128]{1,0:T(8,128)(2,1)S(1)}, bf16[656,128]{1,0:T(8,128)(2,1)S(1)}, u32[]{:S(2)}, u32[]{:S(2)}) collective-permute-start(bf16[656,128]{1,0:T(8,128)(2,1)S(1)} %get-tuple-element.26), channel_id=1, source_target_pairs={{0,2},{2,0},{4,6},{6,4},{8,10},{10,8},{12,14},{14,12},{16,18},{18,... | collective-permute-start | bytes 503816 | tf_op jit(solution)/shard_map/ppermute | solution.py:345
  11.0 4.1 %collective-permute-done.1.got_ref = bf16[656,128]{1,0:T(8,128)(2,1)S(1)} collective-permute-done((bf16[656,128]{1,0:T(8,128)(2,1)S(1)}, bf16[656,128]{1,0:T(8,128)(2,1)S(1)}, u32[]{:S(2)}, u32[]{:S(2)}) %collective-permute-start.1) | collective-permute-done | bytes 167968 | tf_op jit(solution)/shard_map/ppermute | solution.py:345
  15.0 2.0 %level_0.1 = (f32[8,64]{1,0:T(8,128)S(1)}, f32[8,64]{1,0:T(8,128)S(1)}, bf16[832,128]{1,0:T(8,128)(2,1)S(1)}) custom-call(bf16[512,512]{1,0:T(8,128)(2,1)S(1)} %bitcast.11, s32[8,8,128]{2,1,0:T(8,128)S(1)} %get-tuple-element.22.cols_ref, f32[4,4,64,128]{3,2,1,0:T(8,128)S(1)} %get-tuple-element.23.tiles_ref, f32[8,64]{1,0:T(8,128)S(1)} %get-tuple-element.25.rows_ref, ...), custom_call_target="tpu_custom_call" | custom-call | tf_op jit(solution)/shard_map/level_0/pallas_call | solution.py:327
  17.0 12.4 %all_to_all.33 = bf16[4,208,128]{2,1,0:T(8,128)(2,1)S(1)} all-to-all(bf16[4,208,128]{2,1,0:T(8,128)(2,1)S(1)} %bitcast.19), channel_id=1, replica_groups={{0,2,4,6},{8,10,12,14},{16,18,20,22},{24,26,28,30},{1,3,5,7},{9,11,13,1..., dimensions={0} | all-to-all | bytes 425984 | tf_op jit(solution)/shard_map/all_to_all | solution.py:341
  29.4 2.0 %level_1.1 = (f32[8,64]{1,0:T(8,128)S(1)}, f32[8,64]{1,0:T(8,128)S(1)}, bf16[896,128]{1,0:T(8,128)(2,1)S(1)}) custom-call(bf16[512,512]{1,0:T(8,128)(2,1)S(1)} %bitcast.12, s32[8,8,128]{2,1,0:T(8,128)S(1)} %get-tuple-element.22.cols_ref, f32[4,4,64,128]{3,2,1,0:T(8,128)S(1)} %get-tuple-element.23.tiles_ref, bf16[832,128]{1,0:T(8,128)(2,1)S(1)} %bitcast.15, ...), custom_call_target="tpu_custom_call" | custom-call | tf_op jit(solution)/shard_map/level_1/pallas_call | solution.py:327
  31.4 21.9 %all_to_all.34 = bf16[8,112,128]{2,1,0:T(8,128)(2,1)S(1)} all-to-all(bf16[8,112,128]{2,1,0:T(8,128)(2,1)S(1)} %bitcast.18), channel_id=1, replica_groups={{0,2,4,6,8,10,12,14},{16,18,20,22,24,26,28,30},{1,3,5,7,9,11,13,15},{17..., dimensions={0} | all-to-all | bytes 458752 | tf_op jit(solution)/shard_map/all_to_all | solution.py:341
  53.3 2.0 %level_2.1 = (f32[8,64]{1,0:T(8,128)S(1)}, f32[8,64]{1,0:T(8,128)S(1)}, f32[32,128]{1,0:T(8,128)S(1)}, bf16[48,128]{1,0:T(8,128)(2,1)S(1)}) custom-call(bf16[512,512]{1,0:T(8,128)(2,1)S(1)} %bitcast.13, s32[8,8,128]{2,1,0:T(8,128)S(1)} %get-tuple-element.22.cols_ref, bf16[896,128]{1,0:T(8,128)(2,1)S(1)} %bitcast.14, ...), custom_call_target="tpu_custom_call" | custom-call | tf_op jit(solution)/shard_map/level_2/pallas_call | solution.py:327
  55.3 15.7 %collective-permute-start.2 = (bf16[48,128]{1,0:T(8,128)(2,1)S(1)}, bf16[48,128]{1,0:T(8,128)(2,1)S(1)}, u32[]{:S(2)}, u32[]{:S(2)}) collective-permute-start(bf16[48,128]{1,0:T(8,128)(2,1)S(1)} %get-tuple-element.37), channel_id=1, source_target_pairs={{0,16},{2,18},{4,20},{6,22},{8,24},{10,26},{12,28},{14,30},{16,0},... | collective-permute-start | bytes 36872 | tf_op jit(solution)/shard_map/ppermute | solution.py:345
  71.1 1.7 %collective-permute-done.2.got_ref = bf16[48,128]{1,0:T(8,128)(2,1)S(1)} collective-permute-done((bf16[48,128]{1,0:T(8,128)(2,1)S(1)}, bf16[48,128]{1,0:T(8,128)(2,1)S(1)}, u32[]{:S(2)}, u32[]{:S(2)}) %collective-permute-start.2) | collective-permute-done | bytes 12320 | tf_op jit(solution)/shard_map/ppermute | solution.py:345
  72.7 0.1 join.1
  72.9 16.4 %all_to_all.35 = bf16[8,48,128]{2,1,0:T(8,128)(2,1)S(1)} all-to-all(bf16[8,48,128]{2,1,0:T(8,128)(2,1)S(1)} %bitcast.17), channel_id=1, replica_groups={{0,2,4,6,8,10,12,14},{16,18,20,22,24,26,28,30},{1,3,5,7,9,11,13,15},{17..., dimensions={0} | all-to-all | bytes 196608 | tf_op jit(solution)/shard_map/all_to_all | solution.py:341
  89.3 2.2 %level_3.1 = f32[8,64]{1,0:T(8,128)} custom-call(s32[8,8,128]{2,1,0:T(8,128)S(1)} %get-tuple-element.22.cols_ref, bf16[384,128]{1,0:T(8,128)(2,1)S(1)} %bitcast.16, f32[8,64]{1,0:T(8,128)S(1)} %get-tuple-element.38.total_ref), custom_call_target="tpu_custom_call" | custom-call | tf_op jit(solution)/shard_map/level_3/pallas_call | solution.py:327
Async XLA Ops:
  0.0 1.0 %copy-start = (bf16[8,64,512]{2,1,0:T(8,128)(2,1)S(1)}, bf16[8,64,512]{2,1,0:T(8,128)(2,1)}, u32[]{:S(2)}) copy-start(bf16[8,64,512]{2,1,0:T(8,128)(2,1)} %param.6) | copy-start | bytes 1572868
  1.0 0.7 copy-start.2
  1.7 3.5 %copy-start.1 = (bf16[8,64,512]{2,1,0:T(8,128)(2,1)S(1)}, bf16[8,64,512]{2,1,0:T(8,128)(2,1)}, u32[]{:S(2)}) copy-start(bf16[8,64,512]{2,1,0:T(8,128)(2,1)} %param.6) | copy-start | bytes 1572868
  1.7 3.5 %copy-start.3 = (s32[8,6]{1,0:T(8,128)S(1)}, s32[8,6]{1,0:T(8,128)}, u32[]{:S(2)}) copy-start(s32[8,6]{1,0:T(8,128)} %near_ref.1) | copy-start | bytes 580
  3.3 1.9 %copy-start.4 = (s32[1,3,8]{2,0,1:T(1,128)S(1)}, s32[1,3,8]{2,0,1:T(1,128)}, u32[]{:S(2)}) copy-start(s32[1,3,8]{2,0,1:T(1,128)} %param.9) | copy-start | bytes 292
  3.3 1.9 %copy-start.5 = (s32[8]{0:T(128)S(1)}, s32[8]{0:T(128)}, u32[]{:S(2)}) copy-start(s32[8]{0:T(128)} %fine_map_ref.1) | copy-start | bytes 100
  3.3 3.4 %collective-permute-start = (bf16[8,64]{1,0:T(8,128)(2,1)S(1)}, bf16[8,64]{1,0:T(8,128)(2,1)S(1)}, u32[]{:S(2)}, u32[]{:S(2)}) collective-permute-start(bf16[8,64]{1,0:T(8,128)(2,1)S(1)} %get-tuple-element.24.rounded_ref), channel_id=1, source_target_pairs={{0,1},{2,3},{4,5},{6,7},{8,9},{10,11},{12,13},{14,15},{16,17},{18,... | collective-permute-start | bytes 3080 | tf_op jit(solution)/shard_map/ppermute | solution.py:352
  7.2 7.9 %collective-permute-start.1 = (bf16[656,128]{1,0:T(8,128)(2,1)S(1)}, bf16[656,128]{1,0:T(8,128)(2,1)S(1)}, u32[]{:S(2)}, u32[]{:S(2)}) collective-permute-start(bf16[656,128]{1,0:T(8,128)(2,1)S(1)} %get-tuple-element.26), channel_id=1, source_target_pairs={{0,2},{2,0},{4,6},{6,4},{8,10},{10,8},{12,14},{14,12},{16,18},{18,... | collective-permute-start | bytes 503816 | tf_op jit(solution)/shard_map/ppermute | solution.py:345
  55.3 17.4 %collective-permute-start.2 = (bf16[48,128]{1,0:T(8,128)(2,1)S(1)}, bf16[48,128]{1,0:T(8,128)(2,1)S(1)}, u32[]{:S(2)}, u32[]{:S(2)}) collective-permute-start(bf16[48,128]{1,0:T(8,128)(2,1)S(1)} %get-tuple-element.37), channel_id=1, source_target_pairs={{0,16},{2,18},{4,20},{6,22},{8,24},{10,26},{12,28},{14,30},{16,0},... | collective-permute-start | bytes 36872 | tf_op jit(solution)/shard_map/ppermute | solution.py:345

commit v4 on v3

--- a/solution.py
+++ b/solution.py
@@ -15,6 +15,7 @@
 WIDE = 2 * BLOCK
 ROWS = COARSE
 GRANT = 12 * 2**20
+FIRST_GRANT = 60 * 2**20
 INTERPRET = False
 
 F32 = jnp.float32
@@ -107,9 +108,9 @@
     y = values + applied(operand(first), values)
     second = [squared(e) for e in first]
     y = y + applied(operand(second), y)
-    fourth = operand([squared(e) for e in second])
-    y = y + applied(fourth, y)
-    y = y + applied(fourth, applied(fourth, y))
+    fourth = [squared(e) for e in second]
+    y = y + applied(operand(fourth), y)
+    y = y + applied(operand([squared(e) for e in fourth]), y)
     return y * inverse
 
 
@@ -135,11 +136,17 @@
     return fold(full[:ROWS] + full[ROWS:])
 
 
-def fine_kernel(ops_ref, resid_ref, smooth_ref, rounded_ref):
+def fine_kernel(ops_hbm, resid_hbm, smooth_ref, rounded_ref, diag_ref, resid_ref, diag_sem, resid_sem):
+    diag_copy = pltpu.make_async_copy(ops_hbm.at[:, :WIDE], diag_ref, diag_sem)
+    resid_copy = pltpu.make_async_copy(resid_hbm, resid_ref, resid_sem)
+    diag_copy.start()
+    resid_copy.start()
+    diag_copy.wait()
+    resid_copy.wait()
     pairs = []
     for q in range(PAIRS):
-        even = ops_ref[2 * q * BLOCK : (2 * q + 1) * BLOCK, :BLOCK].astype(F32)
-        odd = ops_ref[(2 * q + 1) * BLOCK : (2 * q + 2) * BLOCK, :BLOCK].astype(F32)
+        even = diag_ref[2 * q * BLOCK : (2 * q + 1) * BLOCK, :BLOCK].astype(F32)
+        odd = diag_ref[(2 * q + 1) * BLOCK : (2 * q + 2) * BLOCK, :BLOCK].astype(F32)
         pairs.append(jnp.concatenate([even, odd], axis=1))
     out = smooth(pairs, resid_ref[...])
     smooth_ref[...] = out
@@ -194,7 +201,7 @@
 
 HEAD = 2 * ROWS
 HALF = BLOCK // 2
-SEND0 = HEAD + 2 * PAIRS * BLOCK + 2 * BLOCK
+SEND0 = HEAD + PAIRS * BLOCK + 2 * BLOCK
 SEND1 = HEAD + 2 * BLOCK + BLOCK
 SEND2 = HEAD + BLOCK + HALF
 SEND3 = HEAD + HALF
@@ -240,13 +247,8 @@
     rows = restricted(cols_ref[PAIRS][:, :BLOCK], fresid)
     rows_ref[...] = rows
     other = 1 - lax.rem(lax.axis_index("gy"), 2)
-    send_ref[:HEAD + 2 * BLOCK, :] = packed(rows, [(tiles_ref[1, 2 * other + i], 0) for i in range(2)])
-    at = HEAD + 2 * BLOCK
-    for q in range(PAIRS):
-        high, low = split(tiles_ref[0, q])
-        send_ref[at : at + BLOCK, :] = high
-        send_ref[at + BLOCK : at + 2 * BLOCK, :] = low
-        at += 2 * BLOCK
+    parts = [(tiles_ref[0, q], 0) for q in range(PAIRS)] + [(tiles_ref[1, 2 * other + i], 0) for i in range(2)]
+    send_ref[...] = packed(rows, parts)
 
 
 def descend(level, pairs, coarse_rows, ops_ref, cols_ref, fresid_ref, total_ref, fresid_out, total_out):
@@ -261,15 +263,10 @@
 
 def level0_kernel(ops_ref, cols_ref, tiles_ref, rows_ref, got_ref, fresid_ref, total_ref, fresid_out, total_out, send_ref):
     half = lax.rem(lax.axis_index("gy"), 2)
-    at = HEAD + 2 * BLOCK
-    pairs = []
-    for q in range(PAIRS):
-        high = got_ref[at : at + BLOCK, :].astype(F32)
-        low = got_ref[at + BLOCK : at + 2 * BLOCK, :].astype(F32)
-        pairs.append(tiles_ref[0, q] + high + low)
-        at += 2 * BLOCK
+    received = [got_part(got_ref, 0, i, HEAD + i * BLOCK, BLOCK, 0) for i in range(PAIRS + 2)]
+    pairs = [tiles_ref[0, q] + received[q] for q in range(PAIRS)]
     coarse_rows = rows_ref[...] + got_rows(got_ref, 0)
-    summed = [tiles_ref[1, 2 * half + i] + got_part(got_ref, 0, i, HEAD + i * BLOCK, BLOCK, 0) for i in range(2)]
+    summed = [tiles_ref[1, 2 * half + i] + received[PAIRS + i] for i in range(2)]
     rows = descend(0, pairs, coarse_rows, ops_ref, cols_ref, fresid_ref, total_ref, fresid_out, total_out)
     for e in range(4):
         parts = [(summed[0], 0), (summed[1], 0), (tiles_ref[2, e], 0)]
@@ -321,17 +318,18 @@
     out_ref[...] = total_ref[...] + picked(cols_ref[PAIRS + 3][:, :BLOCK], out)
 
 
-def call(kernel, name, out_shapes, args, scalars=0, scratch=()):
+def call(kernel, name, out_shapes, args, scalars=0, scratch=(), outside=0, grant=GRANT):
+    hbm = pl.BlockSpec(memory_space=pltpu.HBM)
     vmem = pl.BlockSpec(memory_space=pltpu.VMEM)
     smem = pl.BlockSpec(memory_space=pltpu.SMEM)
     return pl.pallas_call(
         kernel,
         name=name,
         out_shape=[jax.ShapeDtypeStruct(shape, kind) for shape, kind in out_shapes],
-        in_specs=[smem] * scalars + [vmem] * (len(args) - scalars),
+        in_specs=[smem] * scalars + [hbm] * outside + [vmem] * (len(args) - scalars - outside),
         out_specs=[vmem] * len(out_shapes),
         scratch_shapes=list(scratch),
-        compiler_params=pltpu.CompilerParams(vmem_limit_bytes=GRANT),
+        compiler_params=pltpu.CompilerParams(vmem_limit_bytes=grant),
         interpret=INTERPRET,
     )(*args)
 
@@ -348,7 +346,20 @@
 def on_device(residual, fine_ops, neighbours, fine_map, coarse_maps):
     ops = fine_ops.reshape(FINE_BLOCKS * BLOCK, SLOTS * BLOCK)
     vec = (FINE_BLOCKS, BLOCK)
-    fine_smooth, rounded = call(fine_kernel, "fine_smooth", [(vec, F32), (vec, BF16)], [ops, residual])
+    fine_smooth, rounded = call(
+        fine_kernel,
+        "fine_smooth",
+        [(vec, F32), (vec, BF16)],
+        [ops, residual],
+        outside=2,
+        grant=FIRST_GRANT,
+        scratch=[
+            pltpu.VMEM((FINE_BLOCKS * BLOCK, WIDE), BF16),
+            pltpu.VMEM(vec, F32),
+            pltpu.SemaphoreType.DMA,
+            pltpu.SemaphoreType.DMA,
+        ],
+    )
     earlier = lax.ppermute(rounded, "ta", [(0, 1)])
     cols, tiles = call(
         tiles_kernel,

time: 91.9 us -> 89.1 us (0.970)
  the two profiles are of different devices: /device:TPU:26 before, /device:TPU:28 now
where the time goes in v4:
time: 89.1 us; the launch traced here: 88.8 us
  blocking collectives  49.8 us (56%)
  starting transfers between devices  21.7 us (24%)
  Pallas kernels  12.1 us (14%)
  waiting for transfers between devices  4.39 us (5%)
    all_to_all x3, blocking collectives, shared(): lax.all_to_all(chunks, 'gy', 0, 0, axis_index_groups=lists, tiled=True)  49.8 us
    ppermute x2, starting transfers between devices, crossed(): lax.ppermute(value, 'gy', [(i, i ^ distance) for i in range(lax.axis_size...  19.9 us
    pallas_call x8, Pallas kernels, call(): pl.pallas_call(kernel, name=name, out_shape=[jax.ShapeDtypeStruct(shape,...  12.1 us
    ppermute x2, waiting for transfers between devices, crossed(): lax.ppermute(value, 'gy', [(i, i ^ distance) for i in range(lax.axis_size...  4.39 us
  transfers between devices with their start and end apart: 3, of which 2 were waited for; matrix products, arithmetic and copies ran while one was open for 0% of the time, Pallas kernels for 2%

profile of v4, /device:TPU:28, one launch (start us, length us, event | category | flops | bytes accessed | tf_op | source)
XLA Modules:
  0.0 88.8 jit_solution(15066549327837972841)
XLA Ops:
  0.0 0.0 copy-start
  0.0 0.0 copy-start.2
  0.0 2.9 %fine_smooth.1 = (f32[8,64]{1,0:T(8,128)}, bf16[8,64]{1,0:T(8,128)(2,1)}) custom-call(bf16[512,512]{1,0:T(8,128)(2,1)} %bitcast.8, f32[8,64]{1,0:T(8,128)} %resid_ref.1), custom_call_target="tpu_custom_call" | custom-call | tf_op jit(solution)/shard_map/fine_smooth/pallas_call | solution.py:325
  2.9 0.0 copy-start.5
  2.9 0.0 copy-start.6
  3.0 1.7 %collective-permute-start = (bf16[8,64]{1,0:T(8,128)(2,1)}, bf16[8,64]{1,0:T(8,128)(2,1)S(1)}, u32[]{:S(2)}, u32[]{:S(2)}) collective-permute-start(bf16[8,64]{1,0:T(8,128)(2,1)} %get-tuple-element.24.rounded_ref), channel_id=1, source_target_pairs={{0,1},{2,3},{4,5},{6,7},{8,9},{10,11},{12,13},{14,15},{16,17},{18,... | collective-permute-start | bytes 3080 | tf_op jit(solution)/shard_map/ppermute | solution.py:363
  4.7 0.0 copy-done
  4.7 0.0 copy-done.2
  4.7 0.0 copy-done.5
  4.7 0.0 copy-done.6
  4.7 0.0 copy-start.1
  4.8 1.5 %tile_parts.1 = (s32[8,8,128]{2,1,0:T(8,128)S(1)}, f32[4,4,64,128]{3,2,1,0:T(8,128)S(1)}) custom-call(s32[8,6]{1,0:T(8,128)S(1)} %copy-done.2, s32[8]{0:T(128)S(1)} %copy-done.6, s32[3,1,8]{2,1,0:T(1,128)S(1)} %bitcast.20, bf16[512,512]{1,0:T(8,128)(2,1)S(1)} %bitcast.9), custom_call_target="tpu_custom_call" | custom-call | tf_op jit(solution)/shard_map/tile_parts/pallas_call | solution.py:325
  6.2 0.0 copy-start.4
  6.2 0.0 collective-permute-done.earlier_ref
  6.2 0.0 copy-done.1
  6.3 0.6 copy-done.4
  6.9 0.4 fine_resid.1
  7.3 0.0 copy-start.3
  7.3 4.0 %collective-permute-start.1 = (bf16[400,128]{1,0:T(8,128)(2,1)S(1)}, bf16[400,128]{1,0:T(8,128)(2,1)S(1)}, u32[]{:S(2)}, u32[]{:S(2)}) collective-permute-start(bf16[400,128]{1,0:T(8,128)(2,1)S(1)} %get-tuple-element.26), channel_id=1, source_target_pairs={{0,2},{2,0},{4,6},{6,4},{8,10},{10,8},{12,14},{14,12},{16,18},{18,... | collective-permute-start | bytes 307208 | tf_op jit(solution)/shard_map/ppermute | solution.py:343
  11.3 2.7 %collective-permute-done.1.got_ref = bf16[400,128]{1,0:T(8,128)(2,1)S(1)} collective-permute-done((bf16[400,128]{1,0:T(8,128)(2,1)S(1)}, bf16[400,128]{1,0:T(8,128)(2,1)S(1)}, u32[]{:S(2)}, u32[]{:S(2)}) %collective-permute-start.1) | collective-permute-done | bytes 102432 | tf_op jit(solution)/shard_map/ppermute | solution.py:343
  14.0 0.0 copy-done.3
  14.0 1.7 %level_0.1 = (f32[8,64]{1,0:T(8,128)S(1)}, f32[8,64]{1,0:T(8,128)S(1)}, bf16[832,128]{1,0:T(8,128)(2,1)S(1)}) custom-call(bf16[512,512]{1,0:T(8,128)(2,1)S(1)} %bitcast.11, s32[8,8,128]{2,1,0:T(8,128)S(1)} %get-tuple-element.22.cols_ref, f32[4,4,64,128]{3,2,1,0:T(8,128)S(1)} %get-tuple-element.23.tiles_ref, f32[8,64]{1,0:T(8,128)S(1)} %get-tuple-element.25.rows_ref, ...), custom_call_target="tpu_custom_call" | custom-call | tf_op jit(solution)/shard_map/level_0/pallas_call | solution.py:325
  15.7 12.5 %all_to_all.33 = bf16[4,208,128]{2,1,0:T(8,128)(2,1)S(1)} all-to-all(bf16[4,208,128]{2,1,0:T(8,128)(2,1)S(1)} %bitcast.19), channel_id=1, replica_groups={{0,2,4,6},{8,10,12,14},{16,18,20,22},{24,26,28,30},{1,3,5,7},{9,11,13,1..., dimensions={0} | all-to-all | bytes 425984 | tf_op jit(solution)/shard_map/all_to_all | solution.py:339
  28.3 1.8 %level_1.1 = (f32[8,64]{1,0:T(8,128)S(1)}, f32[8,64]{1,0:T(8,128)S(1)}, bf16[896,128]{1,0:T(8,128)(2,1)S(1)}) custom-call(bf16[512,512]{1,0:T(8,128)(2,1)S(1)} %bitcast.12, s32[8,8,128]{2,1,0:T(8,128)S(1)} %get-tuple-element.22.cols_ref, f32[4,4,64,128]{3,2,1,0:T(8,128)S(1)} %get-tuple-element.23.tiles_ref, bf16[832,128]{1,0:T(8,128)(2,1)S(1)} %bitcast.15, ...), custom_call_target="tpu_custom_call" | custom-call | tf_op jit(solution)/shard_map/level_1/pallas_call | solution.py:325
  30.0 22.8 %all_to_all.34 = bf16[8,112,128]{2,1,0:T(8,128)(2,1)S(1)} all-to-all(bf16[8,112,128]{2,1,0:T(8,128)(2,1)S(1)} %bitcast.18), channel_id=1, replica_groups={{0,2,4,6,8,10,12,14},{16,18,20,22,24,26,28,30},{1,3,5,7,9,11,13,15},{17..., dimensions={0} | all-to-all | bytes 458752 | tf_op jit(solution)/shard_map/all_to_all | solution.py:339
  52.8 1.8 %level_2.1 = (f32[8,64]{1,0:T(8,128)S(1)}, f32[8,64]{1,0:T(8,128)S(1)}, f32[32,128]{1,0:T(8,128)S(1)}, bf16[48,128]{1,0:T(8,128)(2,1)S(1)}) custom-call(bf16[512,512]{1,0:T(8,128)(2,1)S(1)} %bitcast.13, s32[8,8,128]{2,1,0:T(8,128)S(1)} %get-tuple-element.22.cols_ref, bf16[896,128]{1,0:T(8,128)(2,1)S(1)} %bitcast.14, ...), custom_call_target="tpu_custom_call" | custom-call | tf_op jit(solution)/shard_map/level_2/pallas_call | solution.py:325
  54.6 16.0 %collective-permute-start.2 = (bf16[48,128]{1,0:T(8,128)(2,1)S(1)}, bf16[48,128]{1,0:T(8,128)(2,1)S(1)}, u32[]{:S(2)}, u32[]{:S(2)}) collective-permute-start(bf16[48,128]{1,0:T(8,128)(2,1)S(1)} %get-tuple-element.37), channel_id=1, source_target_pairs={{0,16},{2,18},{4,20},{6,22},{8,24},{10,26},{12,28},{14,30},{16,0},... | collective-permute-start | bytes 36872 | tf_op jit(solution)/shard_map/ppermute | solution.py:343
  70.6 1.7 %collective-permute-done.2.got_ref = bf16[48,128]{1,0:T(8,128)(2,1)S(1)} collective-permute-done((bf16[48,128]{1,0:T(8,128)(2,1)S(1)}, bf16[48,128]{1,0:T(8,128)(2,1)S(1)}, u32[]{:S(2)}, u32[]{:S(2)}) %collective-permute-start.2) | collective-permute-done | bytes 12320 | tf_op jit(solution)/shard_map/ppermute | solution.py:343
  72.3 0.1 join.1
  72.4 14.5 %all_to_all.35 = bf16[8,48,128]{2,1,0:T(8,128)(2,1)S(1)} all-to-all(bf16[8,48,128]{2,1,0:T(8,128)(2,1)S(1)} %bitcast.17), channel_id=1, replica_groups={{0,2,4,6,8,10,12,14},{16,18,20,22,24,26,28,30},{1,3,5,7,9,11,13,15},{17..., dimensions={0} | all-to-all | bytes 196608 | tf_op jit(solution)/shard_map/all_to_all | solution.py:339
  86.9 1.9 %level_3.1 = f32[8,64]{1,0:T(8,128)} custom-call(s32[8,8,128]{2,1,0:T(8,128)S(1)} %get-tuple-element.22.cols_ref, bf16[384,128]{1,0:T(8,128)(2,1)S(1)} %bitcast.16, f32[8,64]{1,0:T(8,128)S(1)} %get-tuple-element.38.total_ref), custom_call_target="tpu_custom_call" | custom-call | tf_op jit(solution)/shard_map/level_3/pallas_call | solution.py:325
Async XLA Ops:
  0.0 4.7 %copy-start = (bf16[8,64,512]{2,1,0:T(8,128)(2,1)S(1)}, bf16[8,64,512]{2,1,0:T(8,128)(2,1)}, u32[]{:S(2)}) copy-start(bf16[8,64,512]{2,1,0:T(8,128)(2,1)} %param.6) | copy-start | bytes 1572868
  0.0 4.7 %copy-start.2 = (s32[8,6]{1,0:T(8,128)S(1)}, s32[8,6]{1,0:T(8,128)}, u32[]{:S(2)}) copy-start(s32[8,6]{1,0:T(8,128)} %near_ref.1) | copy-start | bytes 580
  2.9 1.8 %copy-start.5 = (s32[1,3,8]{2,0,1:T(1,128)S(1)}, s32[1,3,8]{2,0,1:T(1,128)}, u32[]{:S(2)}) copy-start(s32[1,3,8]{2,0,1:T(1,128)} %param.9) | copy-start | bytes 292
  2.9 1.8 %copy-start.6 = (s32[8]{0:T(128)S(1)}, s32[8]{0:T(128)}, u32[]{:S(2)}) copy-start(s32[8]{0:T(128)} %fine_map_ref.1) | copy-start | bytes 100
  3.0 3.3 %collective-permute-start = (bf16[8,64]{1,0:T(8,128)(2,1)}, bf16[8,64]{1,0:T(8,128)(2,1)S(1)}, u32[]{:S(2)}, u32[]{:S(2)}) collective-permute-start(bf16[8,64]{1,0:T(8,128)(2,1)} %get-tuple-element.24.rounded_ref), channel_id=1, source_target_pairs={{0,1},{2,3},{4,5},{6,7},{8,9},{10,11},{12,13},{14,15},{16,17},{18,... | collective-permute-start | bytes 3080 | tf_op jit(solution)/shard_map/ppermute | solution.py:363
  4.7 1.5 %copy-start.1 = (f32[8,64]{1,0:T(8,128)S(1)}, f32[8,64]{1,0:T(8,128)}, u32[]{:S(2)}) copy-start(f32[8,64]{1,0:T(8,128)} %resid_ref.1) | copy-start | bytes 6148
  6.2 0.7 copy-start.4
  7.3 6.7 %copy-start.3 = (f32[8,64]{1,0:T(8,128)S(1)}, f32[8,64]{1,0:T(8,128)}, u32[]{:S(2)}) copy-start(f32[8,64]{1,0:T(8,128)} %get-tuple-element.28.total_ref) | copy-start | bytes 6148
  7.3 6.7 %collective-permute-start.1 = (bf16[400,128]{1,0:T(8,128)(2,1)S(1)}, bf16[400,128]{1,0:T(8,128)(2,1)S(1)}, u32[]{:S(2)}, u32[]{:S(2)}) collective-permute-start(bf16[400,128]{1,0:T(8,128)(2,1)S(1)} %get-tuple-element.26), channel_id=1, source_target_pairs={{0,2},{2,0},{4,6},{6,4},{8,10},{10,8},{12,14},{14,12},{16,18},{18,... | collective-permute-start | bytes 307208 | tf_op jit(solution)/shard_map/ppermute | solution.py:343
  54.6 17.7 %collective-permute-start.2 = (bf16[48,128]{1,0:T(8,128)(2,1)S(1)}, bf16[48,128]{1,0:T(8,128)(2,1)S(1)}, u32[]{:S(2)}, u32[]{:S(2)}) collective-permute-start(bf16[48,128]{1,0:T(8,128)(2,1)S(1)} %get-tuple-element.37), channel_id=1, source_target_pairs={{0,16},{2,18},{4,20},{6,22},{8,24},{10,26},{12,28},{14,30},{16,0},... | collective-permute-start | bytes 36872 | tf_op jit(solution)/shard_map/ppermute | solution.py:343

commit v5 on v4

--- a/solution.py
+++ b/solution.py
@@ -15,7 +15,7 @@
 WIDE = 2 * BLOCK
 ROWS = COARSE
 GRANT = 12 * 2**20
-FIRST_GRANT = 60 * 2**20
+FIRST_GRANT = 55224 * 2**10
 INTERPRET = False
 
 F32 = jnp.float32
@@ -153,50 +153,67 @@
     rounded_ref[...] = out.astype(BF16)
 
 
-def tiles_kernel(near_ref, fine_map_ref, maps_ref, ops_ref, cols_ref, tiles_ref, acc_ref):
+def tiles_kernel(near_ref, fine_map_ref, maps_ref, ops_ref, cols_ref, tiles_ref, acc_ref, labels_ref):
     acc_ref[...] = jnp.zeros_like(acc_ref)
-    left = iota((1, WIDE), 1) < BLOCK
+    left = iota((BLOCK, WIDE), 1) < BLOCK
+    unit = (iota((BLOCK, WIDE), 0) == iota((BLOCK, WIDE), 1) % BLOCK).astype(F32).astype(BF16)
+    digits = [jnp.where(left, 7 * 8 ** (2 * t), 7 * 8 ** (2 * t + 1)) for t in range(LEVELS // 2)]
     rows = iota((ROWS, WIDE), 0)
     first_half = iota((ROWS, WIDE), 1) < BLOCK
 
-    def label(j, level):
-        value = fine_map_ref[j]
-        for step in range(level):
-            value = maps_ref[step, 0, value]
-        return value
+    owns = []
+    for j in range(FINE_BLOCKS):
+        own = [fine_map_ref[j]]
+        for level in range(LEVELS - 1):
+            own.append(maps_ref[level, 0, own[-1]])
+        word = own[0]
+        for level in range(1, LEVELS):
+            word = word + own[level] * 8**level
+        labels_ref[j] = word
+        owns.append((own, word))
 
     index = [jnp.where(first_half, rows, -1)] + [jnp.full((ROWS, WIDE), -1, I32) for q in range(PAIRS - 1)]
     level_cols = [jnp.zeros((ROWS, WIDE), I32) for level in range(LEVELS)]
     for j in range(FINE_BLOCKS):
-        own = [label(j, level) for level in range(LEVELS)]
+        own, word = owns[j]
         others = [near_ref[j, k] for k in range(NEIGHB)]
         for level in range(LEVELS):
             level_cols[level] = jnp.where(rows == j, own[level], level_cols[level])
         for k in range(1, NEIGHB + 1):
             here = (rows == j) & (first_half if k % 2 == 0 else ~first_half)
             index[k // 2] = jnp.where(here, others[k - 1], index[k // 2])
-        tiles = [
-            ops_ref[j * BLOCK : (j + 1) * BLOCK, q * WIDE : (q + 1) * WIDE].astype(F32) for q in range(PAIRS)
-        ]
+        weights = []
+        for k in range(SLOTS):
+            if k > NEIGHB:
+                weights.append(jnp.zeros((BLOCK, LEVELS * BLOCK), BF16))
+                continue
+            if k == 0:
+                weights.append(jnp.concatenate([unit] * (LEVELS // 2), axis=1))
+                continue
+            apart = jnp.full((BLOCK, WIDE), word ^ labels_ref[others[k - 1]], I32)
+            weights.append(
+                jnp.concatenate(
+                    [
+                        unit * jnp.where((apart & digits[t]) == 0, F32(1.0), F32(0.0)).astype(BF16)
+                        for t in range(LEVELS // 2)
+                    ],
+                    axis=1,
+                )
+            )
+        total = product(ops_ref[j * BLOCK : (j + 1) * BLOCK, :], jnp.concatenate(weights, axis=0))
         for level in range(LEVELS):
-            same = [F32(1.0)] + [
-                jnp.where(label(others[k], level) == own[level], F32(1.0), F32(0.0)) for k in range(NEIGHB)
-            ]
-            total = None
-            for q in range(PAIRS):
-                odd = same[2 * q + 1] if 2 * q + 1 <= NEIGHB else F32(0.0)
-                part = tiles[q] * jnp.where(left, same[2 * q], odd)
-                total = part if total is None else total + part
-            acc_ref[level, own[level]] = acc_ref[level, own[level]] + total
+            lanes = slice(level // 2 * WIDE, (level // 2 + 1) * WIDE)
+            mine = left if level % 2 == 0 else ~left
+            acc_ref[own[level], :, lanes] = acc_ref[own[level], :, lanes] + jnp.where(mine, total[:, lanes], 0.0)
     for q in range(PAIRS):
         cols_ref[q] = index[q]
     for level in range(LEVELS):
         cols_ref[PAIRS + level] = level_cols[level]
+    for t in range(LEVELS // 2):
         for q in range(PAIRS):
-            even, odd = acc_ref[level, 2 * q], acc_ref[level, 2 * q + 1]
-            wide_left = iota((BLOCK, WIDE), 1) < BLOCK
-            moved = pltpu.roll(jnp.where(wide_left, odd, even), BLOCK, 1)
-            tiles_ref[level, q] = jnp.where(wide_left, even, odd) + moved
+            even, odd = (acc_ref[2 * q + i, :, t * WIDE : (t + 1) * WIDE] for i in range(2))
+            tiles_ref[2 * t, q] = jnp.where(left, even, pltpu.roll(odd, BLOCK, 1))
+            tiles_ref[2 * t + 1, q] = jnp.where(left, pltpu.roll(even, BLOCK, 1), odd)
 
 
 HEAD = 2 * ROWS
@@ -367,7 +384,7 @@
         [((PAIRS + LEVELS, ROWS, WIDE), I32), ((LEVELS, PAIRS, BLOCK, WIDE), F32)],
         [neighbours, fine_map, jnp.transpose(coarse_maps, (1, 0, 2)), ops],
         scalars=3,
-        scratch=[pltpu.VMEM((LEVELS, COARSE, BLOCK, WIDE), F32)],
+        scratch=[pltpu.VMEM((COARSE, BLOCK, LEVELS * BLOCK), F32), pltpu.SMEM((FINE_BLOCKS,), I32)],
     )
     fresid, rows, sent = call(
         resid_kernel,

time: 89.1 us -> 87.9 us (0.987)
  the two profiles are of different devices: /device:TPU:28 before, /device:TPU:12 now
where the time goes in v5:
time: 87.9 us; the launch traced here: 87.6 us
  blocking collectives  50.4 us (57%)
  starting transfers between devices  21.3 us (24%)
  Pallas kernels  11.5 us (13%)
  waiting for transfers between devices  4.39 us (5%)
    all_to_all x3, blocking collectives, shared(): lax.all_to_all(chunks, 'gy', 0, 0, axis_index_groups=lists, tiled=True)  50.4 us
    ppermute x2, starting transfers between devices, crossed(): lax.ppermute(value, 'gy', [(i, i ^ distance) for i in range(lax.axis_size...  19.5 us
    pallas_call x8, Pallas kernels, call(): pl.pallas_call(kernel, name=name, out_shape=[jax.ShapeDtypeStruct(shape,...  11.5 us
    ppermute x2, waiting for transfers between devices, crossed(): lax.ppermute(value, 'gy', [(i, i ^ distance) for i in range(lax.axis_size...  4.39 us
  transfers between devices with their start and end apart: 3, of which 2 were waited for; matrix products, arithmetic and copies ran while one was open for 0% of the time, Pallas kernels for 2%

profile of v5, /device:TPU:12, one launch (start us, length us, event | category | flops | bytes accessed | tf_op | source)
XLA Modules:
  0.0 87.6 jit_solution(12964221909954275626)
XLA Ops:
  0.0 0.0 copy-start
  0.0 0.0 copy-start.2
  0.0 2.3 %fine_smooth.1 = (f32[8,64]{1,0:T(8,128)S(1)}, bf16[8,64]{1,0:T(8,128)(2,1)S(1)}) custom-call(bf16[512,512]{1,0:T(8,128)(2,1)} %bitcast.8, f32[8,64]{1,0:T(8,128)} %resid_ref.1), custom_call_target="tpu_custom_call" | custom-call | tf_op jit(solution)/shard_map/fine_smooth/pallas_call | solution.py:342
  2.3 0.0 copy-start.3
  2.4 0.0 copy-start.4
  2.4 1.7 %collective-permute-start = (bf16[8,64]{1,0:T(8,128)(2,1)S(1)}, bf16[8,64]{1,0:T(8,128)(2,1)S(1)}, u32[]{:S(2)}, u32[]{:S(2)}) collective-permute-start(bf16[8,64]{1,0:T(8,128)(2,1)S(1)} %get-tuple-element.24.rounded_ref), channel_id=1, source_target_pairs={{0,1},{2,3},{4,5},{6,7},{8,9},{10,11},{12,13},{14,15},{16,17},{18,... | collective-permute-start | bytes 3080 | tf_op jit(solution)/shard_map/ppermute | solution.py:380
  4.1 0.0 copy-done
  4.1 0.0 copy-done.2
  4.1 0.0 copy-done.3
  4.1 0.0 copy-done.4
  4.2 0.0 copy-start.1
  4.2 1.4 %tile_parts.1 = (s32[8,8,128]{2,1,0:T(8,128)S(1)}, f32[4,4,64,128]{3,2,1,0:T(8,128)S(1)}) custom-call(s32[8,6]{1,0:T(8,128)S(1)} %copy-done.2, s32[8]{0:T(128)S(1)} %copy-done.4, s32[3,1,8]{2,1,0:T(1,128)S(1)} %bitcast.20, bf16[512,512]{1,0:T(8,128)(2,1)S(1)} %bitcast.9), custom_call_target="tpu_custom_call" | custom-call | tf_op jit(solution)/shard_map/tile_parts/pallas_call | solution.py:342
  5.5 0.0 collective-permute-done.earlier_ref
  5.5 0.0 copy-done.1
  5.6 0.4 fine_resid.1
  6.0 3.8 %collective-permute-start.1 = (bf16[400,128]{1,0:T(8,128)(2,1)S(1)}, bf16[400,128]{1,0:T(8,128)(2,1)S(1)}, u32[]{:S(2)}, u32[]{:S(2)}) collective-permute-start(bf16[400,128]{1,0:T(8,128)(2,1)S(1)} %get-tuple-element.26), channel_id=1, source_target_pairs={{0,2},{2,0},{4,6},{6,4},{8,10},{10,8},{12,14},{14,12},{16,18},{18,... | collective-permute-start | bytes 307208 | tf_op jit(solution)/shard_map/ppermute | solution.py:360
  9.8 2.7 %collective-permute-done.1.got_ref = bf16[400,128]{1,0:T(8,128)(2,1)S(1)} collective-permute-done((bf16[400,128]{1,0:T(8,128)(2,1)S(1)}, bf16[400,128]{1,0:T(8,128)(2,1)S(1)}, u32[]{:S(2)}, u32[]{:S(2)}) %collective-permute-start.1) | collective-permute-done | bytes 102432 | tf_op jit(solution)/shard_map/ppermute | solution.py:360
  12.5 1.7 %level_0.1 = (f32[8,64]{1,0:T(8,128)S(1)}, f32[8,64]{1,0:T(8,128)S(1)}, bf16[832,128]{1,0:T(8,128)(2,1)S(1)}) custom-call(bf16[512,512]{1,0:T(8,128)(2,1)S(1)} %bitcast.11, s32[8,8,128]{2,1,0:T(8,128)S(1)} %get-tuple-element.22.cols_ref, f32[4,4,64,128]{3,2,1,0:T(8,128)S(1)} %get-tuple-element.23.tiles_ref, f32[8,64]{1,0:T(8,128)S(1)} %get-tuple-element.25.rows_ref, ...), custom_call_target="tpu_custom_call" | custom-call | tf_op jit(solution)/shard_map/level_0/pallas_call | solution.py:342
  14.3 12.5 %all_to_all.33 = bf16[4,208,128]{2,1,0:T(8,128)(2,1)S(1)} all-to-all(bf16[4,208,128]{2,1,0:T(8,128)(2,1)S(1)} %bitcast.19), channel_id=1, replica_groups={{0,2,4,6},{8,10,12,14},{16,18,20,22},{24,26,28,30},{1,3,5,7},{9,11,13,1..., dimensions={0} | all-to-all | bytes 425984 | tf_op jit(solution)/shard_map/all_to_all | solution.py:356
  26.8 1.8 %level_1.1 = (f32[8,64]{1,0:T(8,128)S(1)}, f32[8,64]{1,0:T(8,128)S(1)}, bf16[896,128]{1,0:T(8,128)(2,1)S(1)}) custom-call(bf16[512,512]{1,0:T(8,128)(2,1)S(1)} %bitcast.12, s32[8,8,128]{2,1,0:T(8,128)S(1)} %get-tuple-element.22.cols_ref, f32[4,4,64,128]{3,2,1,0:T(8,128)S(1)} %get-tuple-element.23.tiles_ref, bf16[832,128]{1,0:T(8,128)(2,1)S(1)} %bitcast.15, ...), custom_call_target="tpu_custom_call" | custom-call | tf_op jit(solution)/shard_map/level_1/pallas_call | solution.py:342
  28.6 21.4 %all_to_all.34 = bf16[8,112,128]{2,1,0:T(8,128)(2,1)S(1)} all-to-all(bf16[8,112,128]{2,1,0:T(8,128)(2,1)S(1)} %bitcast.18), channel_id=1, replica_groups={{0,2,4,6,8,10,12,14},{16,18,20,22,24,26,28,30},{1,3,5,7,9,11,13,15},{17..., dimensions={0} | all-to-all | bytes 458752 | tf_op jit(solution)/shard_map/all_to_all | solution.py:356
  50.0 1.8 %level_2.1 = (f32[8,64]{1,0:T(8,128)S(1)}, f32[8,64]{1,0:T(8,128)S(1)}, f32[32,128]{1,0:T(8,128)S(1)}, bf16[48,128]{1,0:T(8,128)(2,1)S(1)}) custom-call(bf16[512,512]{1,0:T(8,128)(2,1)S(1)} %bitcast.13, s32[8,8,128]{2,1,0:T(8,128)S(1)} %get-tuple-element.22.cols_ref, bf16[896,128]{1,0:T(8,128)(2,1)S(1)} %bitcast.14, ...), custom_call_target="tpu_custom_call" | custom-call | tf_op jit(solution)/shard_map/level_2/pallas_call | solution.py:342
  51.8 15.7 %collective-permute-start.2 = (bf16[48,128]{1,0:T(8,128)(2,1)S(1)}, bf16[48,128]{1,0:T(8,128)(2,1)S(1)}, u32[]{:S(2)}, u32[]{:S(2)}) collective-permute-start(bf16[48,128]{1,0:T(8,128)(2,1)S(1)} %get-tuple-element.37), channel_id=1, source_target_pairs={{0,16},{2,18},{4,20},{6,22},{8,24},{10,26},{12,28},{14,30},{16,0},... | collective-permute-start | bytes 36872 | tf_op jit(solution)/shard_map/ppermute | solution.py:360
  67.5 1.7 %collective-permute-done.2.got_ref = bf16[48,128]{1,0:T(8,128)(2,1)S(1)} collective-permute-done((bf16[48,128]{1,0:T(8,128)(2,1)S(1)}, bf16[48,128]{1,0:T(8,128)(2,1)S(1)}, u32[]{:S(2)}, u32[]{:S(2)}) %collective-permute-start.2) | collective-permute-done | bytes 12320 | tf_op jit(solution)/shard_map/ppermute | solution.py:360
  69.1 0.1 join.1
  69.3 16.4 %all_to_all.35 = bf16[8,48,128]{2,1,0:T(8,128)(2,1)S(1)} all-to-all(bf16[8,48,128]{2,1,0:T(8,128)(2,1)S(1)} %bitcast.17), channel_id=1, replica_groups={{0,2,4,6,8,10,12,14},{16,18,20,22,24,26,28,30},{1,3,5,7,9,11,13,15},{17..., dimensions={0} | all-to-all | bytes 196608 | tf_op jit(solution)/shard_map/all_to_all | solution.py:356
  85.7 1.9 %level_3.1 = f32[8,64]{1,0:T(8,128)} custom-call(s32[8,8,128]{2,1,0:T(8,128)S(1)} %get-tuple-element.22.cols_ref, bf16[384,128]{1,0:T(8,128)(2,1)S(1)} %bitcast.16, f32[8,64]{1,0:T(8,128)S(1)} %get-tuple-element.38.total_ref), custom_call_target="tpu_custom_call" | custom-call | tf_op jit(solution)/shard_map/level_3/pallas_call | solution.py:342
Async XLA Ops:
  0.0 4.1 %copy-start = (bf16[8,64,512]{2,1,0:T(8,128)(2,1)S(1)}, bf16[8,64,512]{2,1,0:T(8,128)(2,1)}, u32[]{:S(2)}) copy-start(bf16[8,64,512]{2,1,0:T(8,128)(2,1)} %param.6) | copy-start | bytes 1572868
  0.0 4.1 %copy-start.2 = (s32[8,6]{1,0:T(8,128)S(1)}, s32[8,6]{1,0:T(8,128)}, u32[]{:S(2)}) copy-start(s32[8,6]{1,0:T(8,128)} %near_ref.1) | copy-start | bytes 580
  2.3 1.8 %copy-start.3 = (s32[1,3,8]{2,0,1:T(1,128)S(1)}, s32[1,3,8]{2,0,1:T(1,128)}, u32[]{:S(2)}) copy-start(s32[1,3,8]{2,0,1:T(1,128)} %param.9) | copy-start | bytes 292
  2.4 1.8 %copy-start.4 = (s32[8]{0:T(128)S(1)}, s32[8]{0:T(128)}, u32[]{:S(2)}) copy-start(s32[8]{0:T(128)} %fine_map_ref.1) | copy-start | bytes 100
  2.4 3.2 %collective-permute-start = (bf16[8,64]{1,0:T(8,128)(2,1)S(1)}, bf16[8,64]{1,0:T(8,128)(2,1)S(1)}, u32[]{:S(2)}, u32[]{:S(2)}) collective-permute-start(bf16[8,64]{1,0:T(8,128)(2,1)S(1)} %get-tuple-element.24.rounded_ref), channel_id=1, source_target_pairs={{0,1},{2,3},{4,5},{6,7},{8,9},{10,11},{12,13},{14,15},{16,17},{18,... | collective-permute-start | bytes 3080 | tf_op jit(solution)/shard_map/ppermute | solution.py:380
  4.2 1.4 %copy-start.1 = (f32[8,64]{1,0:T(8,128)S(1)}, f32[8,64]{1,0:T(8,128)}, u32[]{:S(2)}) copy-start(f32[8,64]{1,0:T(8,128)} %resid_ref.1) | copy-start | bytes 6148
  6.0 6.6 %collective-permute-start.1 = (bf16[400,128]{1,0:T(8,128)(2,1)S(1)}, bf16[400,128]{1,0:T(8,128)(2,1)S(1)}, u32[]{:S(2)}, u32[]{:S(2)}) collective-permute-start(bf16[400,128]{1,0:T(8,128)(2,1)S(1)} %get-tuple-element.26), channel_id=1, source_target_pairs={{0,2},{2,0},{4,6},{6,4},{8,10},{10,8},{12,14},{14,12},{16,18},{18,... | collective-permute-start | bytes 307208 | tf_op jit(solution)/shard_map/ppermute | solution.py:360
  51.8 17.4 %collective-permute-start.2 = (bf16[48,128]{1,0:T(8,128)(2,1)S(1)}, bf16[48,128]{1,0:T(8,128)(2,1)S(1)}, u32[]{:S(2)}, u32[]{:S(2)}) collective-permute-start(bf16[48,128]{1,0:T(8,128)(2,1)S(1)} %get-tuple-element.37), channel_id=1, source_target_pairs={{0,16},{2,18},{4,20},{6,22},{8,24},{10,26},{12,28},{14,30},{16,0},... | collective-permute-start | bytes 36872 | tf_op jit(solution)/shard_map/ppermute | solution.py:360

commit v6 on v5

--- a/solution.py
+++ b/solution.py
@@ -15,7 +15,6 @@
 WIDE = 2 * BLOCK
 ROWS = COARSE
 GRANT = 12 * 2**20
-FIRST_GRANT = 55224 * 2**10
 INTERPRET = False
 
 F32 = jnp.float32
@@ -54,13 +53,12 @@
 
 
 def spread(values):
-    doubled = twice(values)
-    return jnp.concatenate([jnp.where(own_lanes(q), doubled, 0.0) for q in range(PAIRS)], axis=1)
+    return jnp.concatenate([jnp.where(own_lanes(q), values, 0.0) for q in range(PAIRS)], axis=1)
 
 
 def fold(wide):
     kept = sum(jnp.where(own_lanes(q), wide[:, q * WIDE : (q + 1) * WIDE], 0.0) for q in range(PAIRS))
-    return kept[:, :BLOCK] + kept[:, BLOCK:]
+    return kept + pltpu.roll(kept, BLOCK, 1)
 
 
 def squared(error):
@@ -90,10 +88,10 @@
 def applied(weights, values):
     full = product_nt(split_rows(spread(values)), weights)
     top = full[:ROWS] + full[ROWS:]
-    return top[:, :BLOCK] + top[:, BLOCK:]
-
-
-def smooth(pairs, values):
+    return top + pltpu.roll(top, BLOCK, 1)
+
+
+def smooth_steps(pairs, values):
     eye = iota((BLOCK, WIDE), 0) == iota((BLOCK, WIDE), 1) % BLOCK
     sums = sum(
         jnp.where(own_lanes(q), jnp.sum(jnp.where(eye, pairs[q], 0.0), axis=0, keepdims=True), 0.0)
@@ -107,11 +105,19 @@
         first.append(one - pairs[q] * along)
     y = values + applied(operand(first), values)
     second = [squared(e) for e in first]
+    yield None
     y = y + applied(operand(second), y)
     fourth = [squared(e) for e in second]
+    yield None
     y = y + applied(operand(fourth), y)
-    y = y + applied(operand([squared(e) for e in fourth]), y)
-    return y * inverse
+    eighth = [squared(e) for e in fourth]
+    yield None
+    y = y + applied(operand(eighth), y)
+    yield y * inverse
+
+
+def smooth(pairs, values):
+    return list(smooth_steps(pairs, values))[-1]
 
 
 def picked(index, values):
@@ -136,25 +142,17 @@
     return fold(full[:ROWS] + full[ROWS:])
 
 
-def fine_kernel(ops_hbm, resid_hbm, smooth_ref, rounded_ref, diag_ref, resid_ref, diag_sem, resid_sem):
-    diag_copy = pltpu.make_async_copy(ops_hbm.at[:, :WIDE], diag_ref, diag_sem)
-    resid_copy = pltpu.make_async_copy(resid_hbm, resid_ref, resid_sem)
-    diag_copy.start()
-    resid_copy.start()
-    diag_copy.wait()
-    resid_copy.wait()
-    pairs = []
-    for q in range(PAIRS):
-        even = diag_ref[2 * q * BLOCK : (2 * q + 1) * BLOCK, :BLOCK].astype(F32)
-        odd = diag_ref[(2 * q + 1) * BLOCK : (2 * q + 2) * BLOCK, :BLOCK].astype(F32)
-        pairs.append(jnp.concatenate([even, odd], axis=1))
-    out = smooth(pairs, resid_ref[...])
-    smooth_ref[...] = out
-    rounded_ref[...] = out.astype(BF16)
-
-
-def tiles_kernel(near_ref, fine_map_ref, maps_ref, ops_ref, cols_ref, tiles_ref, acc_ref, labels_ref):
+def first_kernel(*refs):
+    sources, refs = refs[:5], refs[5:]
+    (smooth_ref, rounded_ref, cols_ref, tiles_ref), refs = refs[:4], refs[4:]
+    held, (acc_ref, labels_ref, sems) = refs[:5], refs[5:]
+    copies = [pltpu.make_async_copy(sources[i], held[i], sems.at[i]) for i in range(5)]
+    for copy in copies:
+        copy.start()
+    near_ref, fine_map_ref, maps_ref, ops_ref, resid_ref = held
     acc_ref[...] = jnp.zeros_like(acc_ref)
+    for copy in copies[:3]:
+        copy.wait()
     left = iota((BLOCK, WIDE), 1) < BLOCK
     unit = (iota((BLOCK, WIDE), 0) == iota((BLOCK, WIDE), 1) % BLOCK).astype(F32).astype(BF16)
     digits = [jnp.where(left, 7 * 8 ** (2 * t), 7 * 8 ** (2 * t + 1)) for t in range(LEVELS // 2)]
@@ -172,6 +170,14 @@
         labels_ref[j] = word
         owns.append((own, word))
 
+    for copy in copies[3:]:
+        copy.wait()
+    pairs = []
+    for q in range(PAIRS):
+        even = ops_ref[2 * q * BLOCK : (2 * q + 1) * BLOCK, :BLOCK].astype(F32)
+        odd = ops_ref[(2 * q + 1) * BLOCK : (2 * q + 2) * BLOCK, :BLOCK].astype(F32)
+        pairs.append(jnp.concatenate([even, odd], axis=1))
+    steps = smooth_steps(pairs, twice(resid_ref[...]))
     index = [jnp.where(first_half, rows, -1)] + [jnp.full((ROWS, WIDE), -1, I32) for q in range(PAIRS - 1)]
     level_cols = [jnp.zeros((ROWS, WIDE), I32) for level in range(LEVELS)]
     for j in range(FINE_BLOCKS):
@@ -205,6 +211,10 @@
             lanes = slice(level // 2 * WIDE, (level // 2 + 1) * WIDE)
             mine = left if level % 2 == 0 else ~left
             acc_ref[own[level], :, lanes] = acc_ref[own[level], :, lanes] + jnp.where(mine, total[:, lanes], 0.0)
+        if j % 2 == 1:
+            out = next(steps)
+    smooth_ref[...] = out
+    rounded_ref[...] = out.astype(BF16)
     for q in range(PAIRS):
         cols_ref[q] = index[q]
     for level in range(LEVELS):
@@ -229,8 +239,9 @@
 
 
 def packed(values, parts):
-    head = jnp.concatenate([values.astype(BF16).astype(F32), values - values.astype(BF16).astype(F32)], axis=1)
     rows = iota((ROWS, WIDE), 0)
+    near = values.astype(BF16).astype(F32)
+    head = jnp.where(iota((ROWS, WIDE), 1) < BLOCK, near, values - near)
     lows = jnp.zeros((ROWS, WIDE), F32)
     body = []
     for i, (part, start) in enumerate(parts):
@@ -243,7 +254,7 @@
 
 def got_rows(ref, base):
     head = ref[base : base + HEAD, :].astype(F32)[:ROWS]
-    return head[:, :BLOCK] + head[:, BLOCK:]
+    return head + pltpu.roll(head, BLOCK, 1)
 
 
 def got_part(ref, base, i, at, size, start):
@@ -253,15 +264,15 @@
 
 
 def resid_kernel(ops_ref, resid_ref, rounded_ref, earlier_ref, cols_ref, tiles_ref, fresid_ref, rows_ref, send_ref):
-    own = twice(rounded_ref[...].astype(F32))
-    before = twice(earlier_ref[...].astype(F32))
+    own = rounded_ref[...].astype(F32)
+    before = earlier_ref[...].astype(F32)
     tiles = gathered(cols_ref, own)
     tiles[-1] = jnp.where(iota((ROWS, WIDE), 1) < BLOCK, tiles[-1], before)
     stacked = jnp.concatenate(tiles, axis=1)
     stacked = jnp.concatenate([stacked, jnp.zeros_like(stacked)], axis=0).astype(BF16)
-    fresid = resid_ref[...] - fold(product_nt(stacked, ops_ref[...])[:ROWS])
+    fresid = twice(resid_ref[...]) - fold(product_nt(stacked, ops_ref[...])[:ROWS])
     fresid_ref[...] = fresid
-    rows = restricted(cols_ref[PAIRS][:, :BLOCK], fresid)
+    rows = restricted(cols_ref[PAIRS], fresid)
     rows_ref[...] = rows
     other = 1 - lax.rem(lax.axis_index("gy"), 2)
     parts = [(tiles_ref[0, q], 0) for q in range(PAIRS)] + [(tiles_ref[1, 2 * other + i], 0) for i in range(2)]
@@ -270,12 +281,12 @@
 
 def descend(level, pairs, coarse_rows, ops_ref, cols_ref, fresid_ref, total_ref, fresid_out, total_out):
     out = smooth(pairs, coarse_rows)
-    on_fine = picked(cols_ref[PAIRS + level][:, :BLOCK], out)
+    on_fine = picked(cols_ref[PAIRS + level], out)
     total_out[...] = total_ref[...] + on_fine
-    fresid = fresid_ref[...] - ops_product(ops_ref, gathered(cols_ref, twice(on_fine)))
+    fresid = fresid_ref[...] - ops_product(ops_ref, gathered(cols_ref, on_fine))
     if fresid_out is not None:
         fresid_out[...] = fresid
-    return restricted(cols_ref[PAIRS + level + 1][:, :BLOCK], fresid)
+    return restricted(cols_ref[PAIRS + level + 1], fresid)
 
 
 def level0_kernel(ops_ref, cols_ref, tiles_ref, rows_ref, got_ref, fresid_ref, total_ref, fresid_out, total_out, send_ref):
@@ -332,21 +343,20 @@
     eighths = [got_part(got_ref, e * SEND3, 0, HEAD, HALF, HALF * (e % 2)) for e in range(8)]
     pairs = [jnp.concatenate([eighths[2 * q], eighths[2 * q + 1]], axis=0) for q in range(PAIRS)]
     out = smooth(pairs, coarse_rows)
-    out_ref[...] = total_ref[...] + picked(cols_ref[PAIRS + 3][:, :BLOCK], out)
-
-
-def call(kernel, name, out_shapes, args, scalars=0, scratch=(), outside=0, grant=GRANT):
+    out_ref[...] = (total_ref[...] + picked(cols_ref[PAIRS + 3], out))[:, :BLOCK]
+
+
+def call(kernel, name, out_shapes, args, scratch=(), outside=0):
     hbm = pl.BlockSpec(memory_space=pltpu.HBM)
     vmem = pl.BlockSpec(memory_space=pltpu.VMEM)
-    smem = pl.BlockSpec(memory_space=pltpu.SMEM)
     return pl.pallas_call(
         kernel,
         name=name,
         out_shape=[jax.ShapeDtypeStruct(shape, kind) for shape, kind in out_shapes],
-        in_specs=[smem] * scalars + [hbm] * outside + [vmem] * (len(args) - scalars - outside),
+        in_specs=[hbm] * outside + [vmem] * (len(args) - outside),
         out_specs=[vmem] * len(out_shapes),
         scratch_shapes=list(scratch),
-        compiler_params=pltpu.CompilerParams(vmem_limit_bytes=grant),
+        compiler_params=pltpu.CompilerParams(vmem_limit_bytes=GRANT),
         interpret=INTERPRET,
     )(*args)
 
@@ -362,30 +372,28 @@
 
 def on_device(residual, fine_ops, neighbours, fine_map, coarse_maps):
     ops = fine_ops.reshape(FINE_BLOCKS * BLOCK, SLOTS * BLOCK)
-    vec = (FINE_BLOCKS, BLOCK)
-    fine_smooth, rounded = call(
-        fine_kernel,
-        "fine_smooth",
-        [(vec, F32), (vec, BF16)],
-        [ops, residual],
-        outside=2,
-        grant=FIRST_GRANT,
+    vec = (FINE_BLOCKS, WIDE)
+    fine_smooth, rounded, cols, tiles = call(
+        first_kernel,
+        "first",
+        [(vec, F32), (vec, BF16), ((PAIRS + LEVELS, ROWS, WIDE), I32), ((LEVELS, PAIRS, BLOCK, WIDE), F32)],
+        [
+            pltpu.with_memory_space_constraint(x, pltpu.HBM)
+            for x in (neighbours, fine_map, jnp.transpose(coarse_maps, (1, 0, 2)), ops, residual)
+        ],
+        outside=5,
         scratch=[
-            pltpu.VMEM((FINE_BLOCKS * BLOCK, WIDE), BF16),
-            pltpu.VMEM(vec, F32),
-            pltpu.SemaphoreType.DMA,
-            pltpu.SemaphoreType.DMA,
+            pltpu.SMEM((FINE_BLOCKS, NEIGHB), I32),
+            pltpu.SMEM((FINE_BLOCKS,), I32),
+            pltpu.SMEM((LEVELS - 1, 1, COARSE), I32),
+            pltpu.VMEM((FINE_BLOCKS * BLOCK, SLOTS * BLOCK), BF16),
+            pltpu.VMEM((FINE_BLOCKS, BLOCK), F32),
+            pltpu.VMEM((COARSE, BLOCK, LEVELS * BLOCK), F32),
+            pltpu.SMEM((FINE_BLOCKS,), I32),
+            pltpu.SemaphoreType.DMA((5,)),
         ],
     )
     earlier = lax.ppermute(rounded, "ta", [(0, 1)])
-    cols, tiles = call(
-        tiles_kernel,
-        "tile_parts",
-        [((PAIRS + LEVELS, ROWS, WIDE), I32), ((LEVELS, PAIRS, BLOCK, WIDE), F32)],
-        [neighbours, fine_map, jnp.transpose(coarse_maps, (1, 0, 2)), ops],
-        scalars=3,
-        scratch=[pltpu.VMEM((COARSE, BLOCK, LEVELS * BLOCK), F32), pltpu.SMEM((FINE_BLOCKS,), I32)],
-    )
     fresid, rows, sent = call(
         resid_kernel,
         "fine_resid",
@@ -416,7 +424,7 @@
     got = crossed(sent, 8)
     (chunks,) = call(join_kernel, "join", [((8 * SEND3, WIDE), BF16)], [rows, part, got])
     got = shared(chunks, 8)
-    (out,) = call(level3_kernel, "level_3", [(vec, F32)], [cols, got, total])
+    (out,) = call(level3_kernel, "level_3", [((FINE_BLOCKS, BLOCK), F32)], [cols, got, total])
     return out
 
 

time: 87.9 us -> 89.3 us (1.016)
  the two profiles are of different devices: /device:TPU:12 before, /device:TPU:4 now
where the time goes in v6:
time: 89.3 us; the launch traced here: 89 us
  blocking collectives  53.1 us (59%)
  starting transfers between devices  21.3 us (24%)
  Pallas kernels  8.66 us (10%)
  waiting for transfers between devices  5.84 us (7%)
    all_to_all x3, blocking collectives, shared(): lax.all_to_all(chunks, 'gy', 0, 0, axis_index_groups=lists, tiled=True)  53.1 us
    ppermute x2, starting transfers between devices, crossed(): lax.ppermute(value, 'gy', [(i, i ^ distance) for i in range(lax.axis_size...  19.6 us
    pallas_call x7, Pallas kernels, call(): pl.pallas_call(kernel, name=name, out_shape=[jax.ShapeDtypeStruct(shape,...  8.66 us
    ppermute x2, waiting for transfers between devices, crossed(): lax.ppermute(value, 'gy', [(i, i ^ distance) for i in range(lax.axis_size...  5.03 us
  transfers between devices with their start and end apart: 3, of which 3 were waited for; matrix products, arithmetic and copies ran while one was open for 0% of the time, Pallas kernels for 0%

profile of v6, /device:TPU:4, one launch (start us, length us, event | category | flops | bytes accessed | tf_op | source)
XLA Modules:
  0.0 89.0 jit_solution(12909506933377879665)
XLA Ops:
  0.0 0.0 copy-start
  0.0 2.4 %first.1 = (f32[8,128]{1,0:T(8,128)S(1)}, bf16[8,128]{1,0:T(8,128)(2,1)S(1)}, s32[8,8,128]{2,1,0:T(8,128)S(1)}, f32[4,4,64,128]{3,2,1,0:T(8,128)S(1)}) custom-call(s32[8,6]{1,0:T(8,128)} %refs_0_.1, s32[8]{0:T(128)} %refs_1_.1, s32[3,1,8]{2,1,0:T(1,128)} %bitcast.19, bf16[512,512]{1,0:T(8,128)(2,1)} %bitcast.8, f32[8,64]{1,0:T(8,128)} %resid_ref.1), custom_call_target="tpu_custom_call" | custom-call | tf_op jit(solution)/shard_map/first/pallas_call | solution.py:352
  2.4 0.0 copy-start.1
  2.4 1.7 %collective-permute-start = (bf16[8,128]{1,0:T(8,128)(2,1)S(1)}, bf16[8,128]{1,0:T(8,128)(2,1)S(1)}, u32[]{:S(2)}, u32[]{:S(2)}) collective-permute-start(bf16[8,128]{1,0:T(8,128)(2,1)S(1)} %get-tuple-element.24.rounded_ref), channel_id=1, source_target_pairs={{0,1},{2,3},{4,5},{6,7},{8,9},{10,11},{12,13},{14,15},{16,17},{18,... | collective-permute-start | bytes 6152 | tf_op jit(solution)/shard_map/ppermute | solution.py:396
  4.2 0.8 collective-permute-done.earlier_ref
  5.0 0.0 copy-done
  5.0 0.0 copy-done.1
  5.0 0.3 fine_resid.1
  5.3 3.8 %collective-permute-start.1 = (bf16[400,128]{1,0:T(8,128)(2,1)S(1)}, bf16[400,128]{1,0:T(8,128)(2,1)S(1)}, u32[]{:S(2)}, u32[]{:S(2)}) collective-permute-start(bf16[400,128]{1,0:T(8,128)(2,1)S(1)} %get-tuple-element.26), channel_id=1, source_target_pairs={{0,2},{2,0},{4,6},{6,4},{8,10},{10,8},{12,14},{14,12},{16,18},{18,... | collective-permute-start | bytes 307208 | tf_op jit(solution)/shard_map/ppermute | solution.py:370
  9.2 3.4 %collective-permute-done.1.got_ref = bf16[400,128]{1,0:T(8,128)(2,1)S(1)} collective-permute-done((bf16[400,128]{1,0:T(8,128)(2,1)S(1)}, bf16[400,128]{1,0:T(8,128)(2,1)S(1)}, u32[]{:S(2)}, u32[]{:S(2)}) %collective-permute-start.1) | collective-permute-done | bytes 102432 | tf_op jit(solution)/shard_map/ppermute | solution.py:370
  12.5 1.4 %level_0.1 = (f32[8,128]{1,0:T(8,128)S(1)}, f32[8,128]{1,0:T(8,128)S(1)}, bf16[832,128]{1,0:T(8,128)(2,1)S(1)}) custom-call(bf16[512,512]{1,0:T(8,128)(2,1)S(1)} %bitcast.10, s32[8,8,128]{2,1,0:T(8,128)S(1)} %get-tuple-element.22.cols_ref, f32[4,4,64,128]{3,2,1,0:T(8,128)S(1)} %get-tuple-element.23.tiles_ref, f32[8,128]{1,0:T(8,128)S(1)} %get-tuple-element.25.rows_ref, ...), custom_call_target="tpu_custom_call" | custom-call | tf_op jit(solution)/shard_map/level_0/pallas_call | solution.py:352
  13.9 13.1 %all_to_all.33 = bf16[4,208,128]{2,1,0:T(8,128)(2,1)S(1)} all-to-all(bf16[4,208,128]{2,1,0:T(8,128)(2,1)S(1)} %bitcast.18), channel_id=1, replica_groups={{0,2,4,6},{8,10,12,14},{16,18,20,22},{24,26,28,30},{1,3,5,7},{9,11,13,1..., dimensions={0} | all-to-all | bytes 425984 | tf_op jit(solution)/shard_map/all_to_all | solution.py:366
  27.0 1.4 %level_1.1 = (f32[8,128]{1,0:T(8,128)S(1)}, f32[8,128]{1,0:T(8,128)S(1)}, bf16[896,128]{1,0:T(8,128)(2,1)S(1)}) custom-call(bf16[512,512]{1,0:T(8,128)(2,1)S(1)} %bitcast.11, s32[8,8,128]{2,1,0:T(8,128)S(1)} %get-tuple-element.22.cols_ref, f32[4,4,64,128]{3,2,1,0:T(8,128)S(1)} %get-tuple-element.23.tiles_ref, bf16[832,128]{1,0:T(8,128)(2,1)S(1)} %bitcast.14, ...), custom_call_target="tpu_custom_call" | custom-call | tf_op jit(solution)/shard_map/level_1/pallas_call | solution.py:352
  28.4 23.6 %all_to_all.34 = bf16[8,112,128]{2,1,0:T(8,128)(2,1)S(1)} all-to-all(bf16[8,112,128]{2,1,0:T(8,128)(2,1)S(1)} %bitcast.17), channel_id=1, replica_groups={{0,2,4,6,8,10,12,14},{16,18,20,22,24,26,28,30},{1,3,5,7,9,11,13,15},{17..., dimensions={0} | all-to-all | bytes 458752 | tf_op jit(solution)/shard_map/all_to_all | solution.py:366
  52.0 1.4 %level_2.1 = (f32[8,128]{1,0:T(8,128)S(1)}, f32[8,128]{1,0:T(8,128)S(1)}, f32[32,128]{1,0:T(8,128)S(1)}, bf16[48,128]{1,0:T(8,128)(2,1)S(1)}) custom-call(bf16[512,512]{1,0:T(8,128)(2,1)S(1)} %bitcast.12, s32[8,8,128]{2,1,0:T(8,128)S(1)} %get-tuple-element.22.cols_ref, bf16[896,128]{1,0:T(8,128)(2,1)S(1)} %bitcast.13, ...), custom_call_target="tpu_custom_call" | custom-call | tf_op jit(solution)/shard_map/level_2/pallas_call | solution.py:352
  53.4 15.7 %collective-permute-start.2 = (bf16[48,128]{1,0:T(8,128)(2,1)S(1)}, bf16[48,128]{1,0:T(8,128)(2,1)S(1)}, u32[]{:S(2)}, u32[]{:S(2)}) collective-permute-start(bf16[48,128]{1,0:T(8,128)(2,1)S(1)} %get-tuple-element.37), channel_id=1, source_target_pairs={{0,16},{2,18},{4,20},{6,22},{8,24},{10,26},{12,28},{14,30},{16,0},... | collective-permute-start | bytes 36872 | tf_op jit(solution)/shard_map/ppermute | solution.py:370
  69.1 1.7 %collective-permute-done.2.got_ref = bf16[48,128]{1,0:T(8,128)(2,1)S(1)} collective-permute-done((bf16[48,128]{1,0:T(8,128)(2,1)S(1)}, bf16[48,128]{1,0:T(8,128)(2,1)S(1)}, u32[]{:S(2)}, u32[]{:S(2)}) %collective-permute-start.2) | collective-permute-done | bytes 12320 | tf_op jit(solution)/shard_map/ppermute | solution.py:370
  70.8 0.1 join.1
  70.8 16.4 %all_to_all.35 = bf16[8,48,128]{2,1,0:T(8,128)(2,1)S(1)} all-to-all(bf16[8,48,128]{2,1,0:T(8,128)(2,1)S(1)} %bitcast.16), channel_id=1, replica_groups={{0,2,4,6,8,10,12,14},{16,18,20,22,24,26,28,30},{1,3,5,7,9,11,13,15},{17..., dimensions={0} | all-to-all | bytes 196608 | tf_op jit(solution)/shard_map/all_to_all | solution.py:366
  87.3 1.7 %level_3.1 = f32[8,64]{1,0:T(8,128)} custom-call(s32[8,8,128]{2,1,0:T(8,128)S(1)} %get-tuple-element.22.cols_ref, bf16[384,128]{1,0:T(8,128)(2,1)S(1)} %bitcast.15, f32[8,128]{1,0:T(8,128)S(1)} %get-tuple-element.38.total_ref), custom_call_target="tpu_custom_call" | custom-call | tf_op jit(solution)/shard_map/level_3/pallas_call | solution.py:352
Async XLA Ops:
  0.0 5.0 %copy-start = (bf16[8,64,512]{2,1,0:T(8,128)(2,1)S(1)}, bf16[8,64,512]{2,1,0:T(8,128)(2,1)}, u32[]{:S(2)}) copy-start(bf16[8,64,512]{2,1,0:T(8,128)(2,1)} %param.6) | copy-start | bytes 1572868
  2.4 2.6 %copy-start.1 = (f32[8,64]{1,0:T(8,128)S(1)}, f32[8,64]{1,0:T(8,128)}, u32[]{:S(2)}) copy-start(f32[8,64]{1,0:T(8,128)} %resid_ref.1) | copy-start | bytes 6148
  2.4 2.5 %collective-permute-start = (bf16[8,128]{1,0:T(8,128)(2,1)S(1)}, bf16[8,128]{1,0:T(8,128)(2,1)S(1)}, u32[]{:S(2)}, u32[]{:S(2)}) collective-permute-start(bf16[8,128]{1,0:T(8,128)(2,1)S(1)} %get-tuple-element.24.rounded_ref), channel_id=1, source_target_pairs={{0,1},{2,3},{4,5},{6,7},{8,9},{10,11},{12,13},{14,15},{16,17},{18,... | collective-permute-start | bytes 6152 | tf_op jit(solution)/shard_map/ppermute | solution.py:396
  5.3 7.2 %collective-permute-start.1 = (bf16[400,128]{1,0:T(8,128)(2,1)S(1)}, bf16[400,128]{1,0:T(8,128)(2,1)S(1)}, u32[]{:S(2)}, u32[]{:S(2)}) collective-permute-start(bf16[400,128]{1,0:T(8,128)(2,1)S(1)} %get-tuple-element.26), channel_id=1, source_target_pairs={{0,2},{2,0},{4,6},{6,4},{8,10},{10,8},{12,14},{14,12},{16,18},{18,... | collective-permute-start | bytes 307208 | tf_op jit(solution)/shard_map/ppermute | solution.py:370
  53.4 17.4 %collective-permute-start.2 = (bf16[48,128]{1,0:T(8,128)(2,1)S(1)}, bf16[48,128]{1,0:T(8,128)(2,1)S(1)}, u32[]{:S(2)}, u32[]{:S(2)}) collective-permute-start(bf16[48,128]{1,0:T(8,128)(2,1)S(1)} %get-tuple-element.37), channel_id=1, source_target_pairs={{0,16},{2,18},{4,20},{6,22},{8,24},{10,26},{12,28},{14,30},{16,0},... | collective-permute-start | bytes 36872 | tf_op jit(solution)/shard_map/ppermute | solution.py:370

commit v7 on v5

--- a/solution.py
+++ b/solution.py
@@ -15,7 +15,6 @@
 WIDE = 2 * BLOCK
 ROWS = COARSE
 GRANT = 12 * 2**20
-FIRST_GRANT = 55224 * 2**10
 INTERPRET = False
 
 F32 = jnp.float32
@@ -54,13 +53,12 @@
 
 
 def spread(values):
-    doubled = twice(values)
-    return jnp.concatenate([jnp.where(own_lanes(q), doubled, 0.0) for q in range(PAIRS)], axis=1)
+    return jnp.concatenate([jnp.where(own_lanes(q), values, 0.0) for q in range(PAIRS)], axis=1)
 
 
 def fold(wide):
     kept = sum(jnp.where(own_lanes(q), wide[:, q * WIDE : (q + 1) * WIDE], 0.0) for q in range(PAIRS))
-    return kept[:, :BLOCK] + kept[:, BLOCK:]
+    return kept + pltpu.roll(kept, BLOCK, 1)
 
 
 def squared(error):
@@ -90,7 +88,7 @@
 def applied(weights, values):
     full = product_nt(split_rows(spread(values)), weights)
     top = full[:ROWS] + full[ROWS:]
-    return top[:, :BLOCK] + top[:, BLOCK:]
+    return top + pltpu.roll(top, BLOCK, 1)
 
 
 def smooth(pairs, values):
@@ -148,7 +146,7 @@
         even = diag_ref[2 * q * BLOCK : (2 * q + 1) * BLOCK, :BLOCK].astype(F32)
         odd = diag_ref[(2 * q + 1) * BLOCK : (2 * q + 2) * BLOCK, :BLOCK].astype(F32)
         pairs.append(jnp.concatenate([even, odd], axis=1))
-    out = smooth(pairs, resid_ref[...])
+    out = smooth(pairs, twice(resid_ref[...]))
     smooth_ref[...] = out
     rounded_ref[...] = out.astype(BF16)
 
@@ -229,8 +227,9 @@
 
 
 def packed(values, parts):
-    head = jnp.concatenate([values.astype(BF16).astype(F32), values - values.astype(BF16).astype(F32)], axis=1)
     rows = iota((ROWS, WIDE), 0)
+    near = values.astype(BF16).astype(F32)
+    head = jnp.where(iota((ROWS, WIDE), 1) < BLOCK, near, values - near)
     lows = jnp.zeros((ROWS, WIDE), F32)
     body = []
     for i, (part, start) in enumerate(parts):
@@ -243,7 +242,7 @@
 
 def got_rows(ref, base):
     head = ref[base : base + HEAD, :].astype(F32)[:ROWS]
-    return head[:, :BLOCK] + head[:, BLOCK:]
+    return head + pltpu.roll(head, BLOCK, 1)
 
 
 def got_part(ref, base, i, at, size, start):
@@ -253,15 +252,15 @@
 
 
 def resid_kernel(ops_ref, resid_ref, rounded_ref, earlier_ref, cols_ref, tiles_ref, fresid_ref, rows_ref, send_ref):
-    own = twice(rounded_ref[...].astype(F32))
-    before = twice(earlier_ref[...].astype(F32))
+    own = rounded_ref[...].astype(F32)
+    before = earlier_ref[...].astype(F32)
     tiles = gathered(cols_ref, own)
     tiles[-1] = jnp.where(iota((ROWS, WIDE), 1) < BLOCK, tiles[-1], before)
     stacked = jnp.concatenate(tiles, axis=1)
     stacked = jnp.concatenate([stacked, jnp.zeros_like(stacked)], axis=0).astype(BF16)
-    fresid = resid_ref[...] - fold(product_nt(stacked, ops_ref[...])[:ROWS])
+    fresid = twice(resid_ref[...]) - fold(product_nt(stacked, ops_ref[...])[:ROWS])
     fresid_ref[...] = fresid
-    rows = restricted(cols_ref[PAIRS][:, :BLOCK], fresid)
+    rows = restricted(cols_ref[PAIRS], fresid)
     rows_ref[...] = rows
     other = 1 - lax.rem(lax.axis_index("gy"), 2)
     parts = [(tiles_ref[0, q], 0) for q in range(PAIRS)] + [(tiles_ref[1, 2 * other + i], 0) for i in range(2)]
@@ -270,12 +269,12 @@
 
 def descend(level, pairs, coarse_rows, ops_ref, cols_ref, fresid_ref, total_ref, fresid_out, total_out):
     out = smooth(pairs, coarse_rows)
-    on_fine = picked(cols_ref[PAIRS + level][:, :BLOCK], out)
+    on_fine = picked(cols_ref[PAIRS + level], out)
     total_out[...] = total_ref[...] + on_fine
-    fresid = fresid_ref[...] - ops_product(ops_ref, gathered(cols_ref, twice(on_fine)))
+    fresid = fresid_ref[...] - ops_product(ops_ref, gathered(cols_ref, on_fine))
     if fresid_out is not None:
         fresid_out[...] = fresid
-    return restricted(cols_ref[PAIRS + level + 1][:, :BLOCK], fresid)
+    return restricted(cols_ref[PAIRS + level + 1], fresid)
 
 
 def level0_kernel(ops_ref, cols_ref, tiles_ref, rows_ref, got_ref, fresid_ref, total_ref, fresid_out, total_out, send_ref):
@@ -332,10 +331,10 @@
     eighths = [got_part(got_ref, e * SEND3, 0, HEAD, HALF, HALF * (e % 2)) for e in range(8)]
     pairs = [jnp.concatenate([eighths[2 * q], eighths[2 * q + 1]], axis=0) for q in range(PAIRS)]
     out = smooth(pairs, coarse_rows)
-    out_ref[...] = total_ref[...] + picked(cols_ref[PAIRS + 3][:, :BLOCK], out)
-
-
-def call(kernel, name, out_shapes, args, scalars=0, scratch=(), outside=0, grant=GRANT):
+    out_ref[...] = (total_ref[...] + picked(cols_ref[PAIRS + 3], out))[:, :BLOCK]
+
+
+def call(kernel, name, out_shapes, args, scalars=0, scratch=(), outside=0):
     hbm = pl.BlockSpec(memory_space=pltpu.HBM)
     vmem = pl.BlockSpec(memory_space=pltpu.VMEM)
     smem = pl.BlockSpec(memory_space=pltpu.SMEM)
@@ -346,7 +345,7 @@
         in_specs=[smem] * scalars + [hbm] * outside + [vmem] * (len(args) - scalars - outside),
         out_specs=[vmem] * len(out_shapes),
         scratch_shapes=list(scratch),
-        compiler_params=pltpu.CompilerParams(vmem_limit_bytes=grant),
+        compiler_params=pltpu.CompilerParams(vmem_limit_bytes=GRANT),
         interpret=INTERPRET,
     )(*args)
 
@@ -362,17 +361,16 @@
 
 def on_device(residual, fine_ops, neighbours, fine_map, coarse_maps):
     ops = fine_ops.reshape(FINE_BLOCKS * BLOCK, SLOTS * BLOCK)
-    vec = (FINE_BLOCKS, BLOCK)
+    vec = (FINE_BLOCKS, WIDE)
     fine_smooth, rounded = call(
         fine_kernel,
         "fine_smooth",
         [(vec, F32), (vec, BF16)],
-        [ops, residual],
+        [pltpu.with_memory_space_constraint(x, pltpu.HBM) for x in (ops, residual)],
         outside=2,
-        grant=FIRST_GRANT,
         scratch=[
             pltpu.VMEM((FINE_BLOCKS * BLOCK, WIDE), BF16),
-            pltpu.VMEM(vec, F32),
+            pltpu.VMEM((FINE_BLOCKS, BLOCK), F32),
             pltpu.SemaphoreType.DMA,
             pltpu.SemaphoreType.DMA,
         ],
@@ -416,7 +414,7 @@
     got = crossed(sent, 8)
     (chunks,) = call(join_kernel, "join", [((8 * SEND3, WIDE), BF16)], [rows, part, got])
     got = shared(chunks, 8)
-    (out,) = call(level3_kernel, "level_3", [(vec, F32)], [cols, got, total])
+    (out,) = call(level3_kernel, "level_3", [((FINE_BLOCKS, BLOCK), F32)], [cols, got, total])
     return out
 
 

time: 87.9 us -> 86.3 us (0.982)
  the two profiles are of different devices: /device:TPU:12 before, /device:TPU:28 now
where the time goes in v7:
time: 86.3 us; the launch traced here: 86 us
  blocking collectives  50.4 us (58%)
  starting transfers between devices  21.3 us (25%)
  Pallas kernels  9.76 us (11%)
  waiting for transfers between devices  4.4 us (5%)
    all_to_all x3, blocking collectives, shared(): lax.all_to_all(chunks, 'gy', 0, 0, axis_index_groups=lists, tiled=True)  50.4 us
    ppermute x2, starting transfers between devices, crossed(): lax.ppermute(value, 'gy', [(i, i ^ distance) for i in range(lax.axis_size...  19.5 us
    pallas_call x8, Pallas kernels, call(): pl.pallas_call(kernel, name=name, out_shape=[jax.ShapeDtypeStruct(shape,...  9.76 us
    ppermute x2, waiting for transfers between devices, crossed(): lax.ppermute(value, 'gy', [(i, i ^ distance) for i in range(lax.axis_size...  4.39 us
    ppermute x1, starting transfers between devices, on_device(): earlier = lax.ppermute(rounded, 'ta', [(0, 1)])  1.74 us
  transfers between devices with their start and end apart: 3, of which 2 were waited for; matrix products, arithmetic and copies ran while one was open for 0% of the time, Pallas kernels for 2%

profile of v7, /device:TPU:28, one launch (start us, length us, event | category | flops | bytes accessed | tf_op | source)
XLA Modules:
  0.0 86.0 jit_solution(2435251018377638735)
XLA Ops:
  0.0 0.0 copy-start
  0.0 0.0 copy-start.2
  0.0 2.1 %fine_smooth.1 = (f32[8,128]{1,0:T(8,128)S(1)}, bf16[8,128]{1,0:T(8,128)(2,1)S(1)}) custom-call(bf16[512,512]{1,0:T(8,128)(2,1)} %bitcast.8, f32[8,64]{1,0:T(8,128)} %resid_ref.1), custom_call_target="tpu_custom_call" | custom-call | tf_op jit(solution)/shard_map/fine_smooth/pallas_call | solution.py:341
  2.1 0.0 copy-start.3
  2.2 0.0 copy-start.4
  2.2 1.7 %collective-permute-start = (bf16[8,128]{1,0:T(8,128)(2,1)S(1)}, bf16[8,128]{1,0:T(8,128)(2,1)S(1)}, u32[]{:S(2)}, u32[]{:S(2)}) collective-permute-start(bf16[8,128]{1,0:T(8,128)(2,1)S(1)} %get-tuple-element.24.rounded_ref), channel_id=1, source_target_pairs={{0,1},{2,3},{4,5},{6,7},{8,9},{10,11},{12,13},{14,15},{16,17},{18,... | collective-permute-start | bytes 6152 | tf_op jit(solution)/shard_map/ppermute | solution.py:378
  3.9 0.0 copy-done
  3.9 0.0 copy-done.2
  3.9 0.0 copy-done.3
  3.9 0.0 copy-done.4
  4.0 0.0 copy-start.1
  4.0 1.4 %tile_parts.1 = (s32[8,8,128]{2,1,0:T(8,128)S(1)}, f32[4,4,64,128]{3,2,1,0:T(8,128)S(1)}) custom-call(s32[8,6]{1,0:T(8,128)S(1)} %copy-done.2, s32[8]{0:T(128)S(1)} %copy-done.4, s32[3,1,8]{2,1,0:T(1,128)S(1)} %bitcast.20, bf16[512,512]{1,0:T(8,128)(2,1)S(1)} %bitcast.9), custom_call_target="tpu_custom_call" | custom-call | tf_op jit(solution)/shard_map/tile_parts/pallas_call | solution.py:341
  5.3 0.0 collective-permute-done.earlier_ref
  5.3 0.0 copy-done.1
  5.4 0.3 fine_resid.1
  5.7 3.8 %collective-permute-start.1 = (bf16[400,128]{1,0:T(8,128)(2,1)S(1)}, bf16[400,128]{1,0:T(8,128)(2,1)S(1)}, u32[]{:S(2)}, u32[]{:S(2)}) collective-permute-start(bf16[400,128]{1,0:T(8,128)(2,1)S(1)} %get-tuple-element.26), channel_id=1, source_target_pairs={{0,2},{2,0},{4,6},{6,4},{8,10},{10,8},{12,14},{14,12},{16,18},{18,... | collective-permute-start | bytes 307208 | tf_op jit(solution)/shard_map/ppermute | solution.py:359
  9.5 2.7 %collective-permute-done.1.got_ref = bf16[400,128]{1,0:T(8,128)(2,1)S(1)} collective-permute-done((bf16[400,128]{1,0:T(8,128)(2,1)S(1)}, bf16[400,128]{1,0:T(8,128)(2,1)S(1)}, u32[]{:S(2)}, u32[]{:S(2)}) %collective-permute-start.1) | collective-permute-done | bytes 102432 | tf_op jit(solution)/shard_map/ppermute | solution.py:359
  12.3 1.4 %level_0.1 = (f32[8,128]{1,0:T(8,128)S(1)}, f32[8,128]{1,0:T(8,128)S(1)}, bf16[832,128]{1,0:T(8,128)(2,1)S(1)}) custom-call(bf16[512,512]{1,0:T(8,128)(2,1)S(1)} %bitcast.11, s32[8,8,128]{2,1,0:T(8,128)S(1)} %get-tuple-element.22.cols_ref, f32[4,4,64,128]{3,2,1,0:T(8,128)S(1)} %get-tuple-element.23.tiles_ref, f32[8,128]{1,0:T(8,128)S(1)} %get-tuple-element.25.rows_ref, ...), custom_call_target="tpu_custom_call" | custom-call | tf_op jit(solution)/shard_map/level_0/pallas_call | solution.py:341
  13.6 12.5 %all_to_all.33 = bf16[4,208,128]{2,1,0:T(8,128)(2,1)S(1)} all-to-all(bf16[4,208,128]{2,1,0:T(8,128)(2,1)S(1)} %bitcast.19), channel_id=1, replica_groups={{0,2,4,6},{8,10,12,14},{16,18,20,22},{24,26,28,30},{1,3,5,7},{9,11,13,1..., dimensions={0} | all-to-all | bytes 425984 | tf_op jit(solution)/shard_map/all_to_all | solution.py:355
  26.2 1.4 %level_1.1 = (f32[8,128]{1,0:T(8,128)S(1)}, f32[8,128]{1,0:T(8,128)S(1)}, bf16[896,128]{1,0:T(8,128)(2,1)S(1)}) custom-call(bf16[512,512]{1,0:T(8,128)(2,1)S(1)} %bitcast.12, s32[8,8,128]{2,1,0:T(8,128)S(1)} %get-tuple-element.22.cols_ref, f32[4,4,64,128]{3,2,1,0:T(8,128)S(1)} %get-tuple-element.23.tiles_ref, bf16[832,128]{1,0:T(8,128)(2,1)S(1)} %bitcast.15, ...), custom_call_target="tpu_custom_call" | custom-call | tf_op jit(solution)/shard_map/level_1/pallas_call | solution.py:341
  27.6 21.4 %all_to_all.34 = bf16[8,112,128]{2,1,0:T(8,128)(2,1)S(1)} all-to-all(bf16[8,112,128]{2,1,0:T(8,128)(2,1)S(1)} %bitcast.18), channel_id=1, replica_groups={{0,2,4,6,8,10,12,14},{16,18,20,22,24,26,28,30},{1,3,5,7,9,11,13,15},{17..., dimensions={0} | all-to-all | bytes 458752 | tf_op jit(solution)/shard_map/all_to_all | solution.py:355
  49.0 1.4 %level_2.1 = (f32[8,128]{1,0:T(8,128)S(1)}, f32[8,128]{1,0:T(8,128)S(1)}, f32[32,128]{1,0:T(8,128)S(1)}, bf16[48,128]{1,0:T(8,128)(2,1)S(1)}) custom-call(bf16[512,512]{1,0:T(8,128)(2,1)S(1)} %bitcast.13, s32[8,8,128]{2,1,0:T(8,128)S(1)} %get-tuple-element.22.cols_ref, bf16[896,128]{1,0:T(8,128)(2,1)S(1)} %bitcast.14, ...), custom_call_target="tpu_custom_call" | custom-call | tf_op jit(solution)/shard_map/level_2/pallas_call | solution.py:341
  50.4 15.7 %collective-permute-start.2 = (bf16[48,128]{1,0:T(8,128)(2,1)S(1)}, bf16[48,128]{1,0:T(8,128)(2,1)S(1)}, u32[]{:S(2)}, u32[]{:S(2)}) collective-permute-start(bf16[48,128]{1,0:T(8,128)(2,1)S(1)} %get-tuple-element.37), channel_id=1, source_target_pairs={{0,16},{2,18},{4,20},{6,22},{8,24},{10,26},{12,28},{14,30},{16,0},... | collective-permute-start | bytes 36872 | tf_op jit(solution)/shard_map/ppermute | solution.py:359
  66.1 1.7 %collective-permute-done.2.got_ref = bf16[48,128]{1,0:T(8,128)(2,1)S(1)} collective-permute-done((bf16[48,128]{1,0:T(8,128)(2,1)S(1)}, bf16[48,128]{1,0:T(8,128)(2,1)S(1)}, u32[]{:S(2)}, u32[]{:S(2)}) %collective-permute-start.2) | collective-permute-done | bytes 12320 | tf_op jit(solution)/shard_map/ppermute | solution.py:359
  67.8 0.1 join.1
  67.9 16.4 %all_to_all.35 = bf16[8,48,128]{2,1,0:T(8,128)(2,1)S(1)} all-to-all(bf16[8,48,128]{2,1,0:T(8,128)(2,1)S(1)} %bitcast.17), channel_id=1, replica_groups={{0,2,4,6,8,10,12,14},{16,18,20,22,24,26,28,30},{1,3,5,7,9,11,13,15},{17..., dimensions={0} | all-to-all | bytes 196608 | tf_op jit(solution)/shard_map/all_to_all | solution.py:355
  84.3 1.7 %level_3.1 = f32[8,64]{1,0:T(8,128)} custom-call(s32[8,8,128]{2,1,0:T(8,128)S(1)} %get-tuple-element.22.cols_ref, bf16[384,128]{1,0:T(8,128)(2,1)S(1)} %bitcast.16, f32[8,128]{1,0:T(8,128)S(1)} %get-tuple-element.38.total_ref), custom_call_target="tpu_custom_call" | custom-call | tf_op jit(solution)/shard_map/level_3/pallas_call | solution.py:341
Async XLA Ops:
  0.0 3.9 %copy-start = (bf16[8,64,512]{2,1,0:T(8,128)(2,1)S(1)}, bf16[8,64,512]{2,1,0:T(8,128)(2,1)}, u32[]{:S(2)}) copy-start(bf16[8,64,512]{2,1,0:T(8,128)(2,1)} %param.6) | copy-start | bytes 1572868
  0.0 3.9 %copy-start.2 = (s32[8,6]{1,0:T(8,128)S(1)}, s32[8,6]{1,0:T(8,128)}, u32[]{:S(2)}) copy-start(s32[8,6]{1,0:T(8,128)} %near_ref.1) | copy-start | bytes 580
  2.1 1.8 %copy-start.3 = (s32[1,3,8]{2,0,1:T(1,128)S(1)}, s32[1,3,8]{2,0,1:T(1,128)}, u32[]{:S(2)}) copy-start(s32[1,3,8]{2,0,1:T(1,128)} %param.9) | copy-start | bytes 292
  2.2 1.8 %copy-start.4 = (s32[8]{0:T(128)S(1)}, s32[8]{0:T(128)}, u32[]{:S(2)}) copy-start(s32[8]{0:T(128)} %fine_map_ref.1) | copy-start | bytes 100
  2.2 3.2 %collective-permute-start = (bf16[8,128]{1,0:T(8,128)(2,1)S(1)}, bf16[8,128]{1,0:T(8,128)(2,1)S(1)}, u32[]{:S(2)}, u32[]{:S(2)}) collective-permute-start(bf16[8,128]{1,0:T(8,128)(2,1)S(1)} %get-tuple-element.24.rounded_ref), channel_id=1, source_target_pairs={{0,1},{2,3},{4,5},{6,7},{8,9},{10,11},{12,13},{14,15},{16,17},{18,... | collective-permute-start | bytes 6152 | tf_op jit(solution)/shard_map/ppermute | solution.py:378
  4.0 1.4 %copy-start.1 = (f32[8,64]{1,0:T(8,128)S(1)}, f32[8,64]{1,0:T(8,128)}, u32[]{:S(2)}) copy-start(f32[8,64]{1,0:T(8,128)} %resid_ref.1) | copy-start | bytes 6148
  5.7 6.6 %collective-permute-start.1 = (bf16[400,128]{1,0:T(8,128)(2,1)S(1)}, bf16[400,128]{1,0:T(8,128)(2,1)S(1)}, u32[]{:S(2)}, u32[]{:S(2)}) collective-permute-start(bf16[400,128]{1,0:T(8,128)(2,1)S(1)} %get-tuple-element.26), channel_id=1, source_target_pairs={{0,2},{2,0},{4,6},{6,4},{8,10},{10,8},{12,14},{14,12},{16,18},{18,... | collective-permute-start | bytes 307208 | tf_op jit(solution)/shard_map/ppermute | solution.py:359
  50.4 17.4 %collective-permute-start.2 = (bf16[48,128]{1,0:T(8,128)(2,1)S(1)}, bf16[48,128]{1,0:T(8,128)(2,1)S(1)}, u32[]{:S(2)}, u32[]{:S(2)}) collective-permute-start(bf16[48,128]{1,0:T(8,128)(2,1)S(1)} %get-tuple-element.37), channel_id=1, source_target_pairs={{0,16},{2,18},{4,20},{6,22},{8,24},{10,26},{12,28},{14,30},{16,0},... | collective-permute-start | bytes 36872 | tf_op jit(solution)/shard_map/ppermute | solution.py:359

commit v8 on v7

--- a/solution.py
+++ b/solution.py
@@ -134,11 +134,12 @@
     return fold(full[:ROWS] + full[ROWS:])
 
 
-def fine_kernel(ops_hbm, resid_hbm, smooth_ref, rounded_ref, diag_ref, resid_ref, diag_sem, resid_sem):
+def fine_kernel(ops_hbm, resid_hbm, smooth_ref, rounded_ref, zeros_ref, diag_ref, resid_ref, diag_sem, resid_sem):
     diag_copy = pltpu.make_async_copy(ops_hbm.at[:, :WIDE], diag_ref, diag_sem)
     resid_copy = pltpu.make_async_copy(resid_hbm, resid_ref, resid_sem)
     diag_copy.start()
     resid_copy.start()
+    zeros_ref[...] = jnp.zeros_like(zeros_ref)
     diag_copy.wait()
     resid_copy.wait()
     pairs = []
@@ -151,8 +152,7 @@
     rounded_ref[...] = out.astype(BF16)
 
 
-def tiles_kernel(near_ref, fine_map_ref, maps_ref, ops_ref, cols_ref, tiles_ref, acc_ref, labels_ref):
-    acc_ref[...] = jnp.zeros_like(acc_ref)
+def tiles_kernel(near_ref, fine_map_ref, maps_ref, ops_ref, zeros_ref, cols_ref, tiles_ref, acc_ref, labels_ref):
     left = iota((BLOCK, WIDE), 1) < BLOCK
     unit = (iota((BLOCK, WIDE), 0) == iota((BLOCK, WIDE), 1) % BLOCK).astype(F32).astype(BF16)
     digits = [jnp.where(left, 7 * 8 ** (2 * t), 7 * 8 ** (2 * t + 1)) for t in range(LEVELS // 2)]
@@ -334,7 +334,7 @@
     out_ref[...] = (total_ref[...] + picked(cols_ref[PAIRS + 3], out))[:, :BLOCK]
 
 
-def call(kernel, name, out_shapes, args, scalars=0, scratch=(), outside=0):
+def call(kernel, name, out_shapes, args, scalars=0, scratch=(), outside=0, aliases={}):
     hbm = pl.BlockSpec(memory_space=pltpu.HBM)
     vmem = pl.BlockSpec(memory_space=pltpu.VMEM)
     smem = pl.BlockSpec(memory_space=pltpu.SMEM)
@@ -346,6 +346,7 @@
         out_specs=[vmem] * len(out_shapes),
         scratch_shapes=list(scratch),
         compiler_params=pltpu.CompilerParams(vmem_limit_bytes=GRANT),
+        input_output_aliases=aliases,
         interpret=INTERPRET,
     )(*args)
 
@@ -362,10 +363,11 @@
 def on_device(residual, fine_ops, neighbours, fine_map, coarse_maps):
     ops = fine_ops.reshape(FINE_BLOCKS * BLOCK, SLOTS * BLOCK)
     vec = (FINE_BLOCKS, WIDE)
-    fine_smooth, rounded = call(
+    share = ((COARSE, BLOCK, LEVELS * BLOCK), F32)
+    fine_smooth, rounded, zeros = call(
         fine_kernel,
         "fine_smooth",
-        [(vec, F32), (vec, BF16)],
+        [(vec, F32), (vec, BF16), share],
         [pltpu.with_memory_space_constraint(x, pltpu.HBM) for x in (ops, residual)],
         outside=2,
         scratch=[
@@ -376,13 +378,14 @@
         ],
     )
     earlier = lax.ppermute(rounded, "ta", [(0, 1)])
-    cols, tiles = call(
+    cols, tiles, _ = call(
         tiles_kernel,
         "tile_parts",
-        [((PAIRS + LEVELS, ROWS, WIDE), I32), ((LEVELS, PAIRS, BLOCK, WIDE), F32)],
-        [neighbours, fine_map, jnp.transpose(coarse_maps, (1, 0, 2)), ops],
+        [((PAIRS + LEVELS, ROWS, WIDE), I32), ((LEVELS, PAIRS, BLOCK, WIDE), F32), share],
+        [neighbours, fine_map, jnp.transpose(coarse_maps, (1, 0, 2)), ops, zeros],
         scalars=3,
-        scratch=[pltpu.VMEM((COARSE, BLOCK, LEVELS * BLOCK), F32), pltpu.SMEM((FINE_BLOCKS,), I32)],
+        scratch=[pltpu.SMEM((FINE_BLOCKS,), I32)],
+        aliases={4: 2},
     )
     fresid, rows, sent = call(
         resid_kernel,

time: 86.3 us -> 86.3 us (level)
  the two profiles are of different devices: /device:TPU:28 before, /device:TPU:4 now
where the time goes in v8:
time: 86.3 us; the launch traced here: 86 us
  blocking collectives  50.4 us (58%)
  starting transfers between devices  21.3 us (25%)
  Pallas kernels  9.77 us (11%)
  waiting for transfers between devices  4.38 us (5%)
    all_to_all x3, blocking collectives, shared(): lax.all_to_all(chunks, 'gy', 0, 0, axis_index_groups=lists, tiled=True)  50.4 us
    ppermute x2, starting transfers between devices, crossed(): lax.ppermute(value, 'gy', [(i, i ^ distance) for i in range(lax.axis_size...  19.6 us
    pallas_call x8, Pallas kernels, call(): pl.pallas_call(kernel, name=name, out_shape=[jax.ShapeDtypeStruct(shape,...  9.77 us
    ppermute x2, waiting for transfers between devices, crossed(): lax.ppermute(value, 'gy', [(i, i ^ distance) for i in range(lax.axis_size...  4.37 us
    ppermute x1, starting transfers between devices, on_device(): earlier = lax.ppermute(rounded, 'ta', [(0, 1)])  1.74 us
  transfers between devices with their start and end apart: 3, of which 2 were waited for; matrix products, arithmetic and copies ran while one was open for 0% of the time, Pallas kernels for 2%

profile of v8, /device:TPU:4, one launch (start us, length us, event | category | flops | bytes accessed | tf_op | source)
XLA Modules:
  0.0 86.0 jit_solution(11121264212307363363)
XLA Ops:
  0.0 0.0 copy-start
  0.0 0.0 copy-start.4
  0.0 2.1 %fine_smooth.1 = (f32[8,128]{1,0:T(8,128)S(1)}, bf16[8,128]{1,0:T(8,128)(2,1)S(1)}, f32[8,64,256]{2,1,0:T(8,128)S(1)}) custom-call(bf16[512,512]{1,0:T(8,128)(2,1)} %bitcast.8, f32[8,64]{1,0:T(8,128)} %resid_ref.1), custom_call_target="tpu_custom_call" | custom-call | tf_op jit(solution)/shard_map/fine_smooth/pallas_call | solution.py:341
  2.1 0.0 copy-start.2
  2.2 0.0 copy-start.3
  2.2 1.7 %collective-permute-start = (bf16[8,128]{1,0:T(8,128)(2,1)S(1)}, bf16[8,128]{1,0:T(8,128)(2,1)S(1)}, u32[]{:S(2)}, u32[]{:S(2)}) collective-permute-start(bf16[8,128]{1,0:T(8,128)(2,1)S(1)} %get-tuple-element.26.rounded_ref), channel_id=1, source_target_pairs={{0,1},{2,3},{4,5},{6,7},{8,9},{10,11},{12,13},{14,15},{16,17},{18,... | collective-permute-start | bytes 6152 | tf_op jit(solution)/shard_map/ppermute | solution.py:380
  3.9 0.0 copy-done
  3.9 0.0 copy-done.4
  3.9 0.0 copy-done.2
  3.9 0.0 copy-done.3
  4.0 0.0 copy-start.1
  4.0 1.4 %tile_parts.1 = (s32[8,8,128]{2,1,0:T(8,128)S(1)}, f32[4,4,64,128]{3,2,1,0:T(8,128)S(1)}, f32[8,64,256]{2,1,0:T(8,128)S(1)}) custom-call(s32[8,6]{1,0:T(8,128)S(1)} %copy-done.2, s32[8]{0:T(128)S(1)} %copy-done.4, s32[3,1,8]{2,1,0:T(1,128)S(1)} %bitcast.20, bf16[512,512]{1,0:T(8,128)(2,1)S(1)} %bitcast.9, ...), custom_call_target="tpu_custom_call", output_to_operand_aliasing={{2}: (4, {})} | custom-call | tf_op jit(solution)/shard_map/tile_parts/pallas_call | solution.py:341
  5.3 0.0 collective-permute-done.earlier_ref
  5.4 0.0 copy-done.1
  5.4 0.3 fine_resid.1
  5.7 3.8 %collective-permute-start.1 = (bf16[400,128]{1,0:T(8,128)(2,1)S(1)}, bf16[400,128]{1,0:T(8,128)(2,1)S(1)}, u32[]{:S(2)}, u32[]{:S(2)}) collective-permute-start(bf16[400,128]{1,0:T(8,128)(2,1)S(1)} %get-tuple-element.28), channel_id=1, source_target_pairs={{0,2},{2,0},{4,6},{6,4},{8,10},{10,8},{12,14},{14,12},{16,18},{18,... | collective-permute-start | bytes 307208 | tf_op jit(solution)/shard_map/ppermute | solution.py:360
  9.6 2.7 %collective-permute-done.1.got_ref = bf16[400,128]{1,0:T(8,128)(2,1)S(1)} collective-permute-done((bf16[400,128]{1,0:T(8,128)(2,1)S(1)}, bf16[400,128]{1,0:T(8,128)(2,1)S(1)}, u32[]{:S(2)}, u32[]{:S(2)}) %collective-permute-start.1) | collective-permute-done | bytes 102432 | tf_op jit(solution)/shard_map/ppermute | solution.py:360
  12.3 1.4 %level_0.1 = (f32[8,128]{1,0:T(8,128)S(1)}, f32[8,128]{1,0:T(8,128)S(1)}, bf16[832,128]{1,0:T(8,128)(2,1)S(1)}) custom-call(bf16[512,512]{1,0:T(8,128)(2,1)S(1)} %bitcast.11, s32[8,8,128]{2,1,0:T(8,128)S(1)} %get-tuple-element.24.cols_ref, f32[4,4,64,128]{3,2,1,0:T(8,128)S(1)} %get-tuple-element.25.tiles_ref, f32[8,128]{1,0:T(8,128)S(1)} %get-tuple-element.27.rows_ref, ...), custom_call_target="tpu_custom_call" | custom-call | tf_op jit(solution)/shard_map/level_0/pallas_call | solution.py:341
  13.7 12.5 %all_to_all.33 = bf16[4,208,128]{2,1,0:T(8,128)(2,1)S(1)} all-to-all(bf16[4,208,128]{2,1,0:T(8,128)(2,1)S(1)} %bitcast.19), channel_id=1, replica_groups={{0,2,4,6},{8,10,12,14},{16,18,20,22},{24,26,28,30},{1,3,5,7},{9,11,13,1..., dimensions={0} | all-to-all | bytes 425984 | tf_op jit(solution)/shard_map/all_to_all | solution.py:356
  26.2 1.4 %level_1.1 = (f32[8,128]{1,0:T(8,128)S(1)}, f32[8,128]{1,0:T(8,128)S(1)}, bf16[896,128]{1,0:T(8,128)(2,1)S(1)}) custom-call(bf16[512,512]{1,0:T(8,128)(2,1)S(1)} %bitcast.12, s32[8,8,128]{2,1,0:T(8,128)S(1)} %get-tuple-element.24.cols_ref, f32[4,4,64,128]{3,2,1,0:T(8,128)S(1)} %get-tuple-element.25.tiles_ref, bf16[832,128]{1,0:T(8,128)(2,1)S(1)} %bitcast.15, ...), custom_call_target="tpu_custom_call" | custom-call | tf_op jit(solution)/shard_map/level_1/pallas_call | solution.py:341
  27.6 21.4 %all_to_all.34 = bf16[8,112,128]{2,1,0:T(8,128)(2,1)S(1)} all-to-all(bf16[8,112,128]{2,1,0:T(8,128)(2,1)S(1)} %bitcast.18), channel_id=1, replica_groups={{0,2,4,6,8,10,12,14},{16,18,20,22,24,26,28,30},{1,3,5,7,9,11,13,15},{17..., dimensions={0} | all-to-all | bytes 458752 | tf_op jit(solution)/shard_map/all_to_all | solution.py:356
  49.0 1.4 %level_2.1 = (f32[8,128]{1,0:T(8,128)S(1)}, f32[8,128]{1,0:T(8,128)S(1)}, f32[32,128]{1,0:T(8,128)S(1)}, bf16[48,128]{1,0:T(8,128)(2,1)S(1)}) custom-call(bf16[512,512]{1,0:T(8,128)(2,1)S(1)} %bitcast.13, s32[8,8,128]{2,1,0:T(8,128)S(1)} %get-tuple-element.24.cols_ref, bf16[896,128]{1,0:T(8,128)(2,1)S(1)} %bitcast.14, ...), custom_call_target="tpu_custom_call" | custom-call | tf_op jit(solution)/shard_map/level_2/pallas_call | solution.py:341
  50.4 15.7 %collective-permute-start.2 = (bf16[48,128]{1,0:T(8,128)(2,1)S(1)}, bf16[48,128]{1,0:T(8,128)(2,1)S(1)}, u32[]{:S(2)}, u32[]{:S(2)}) collective-permute-start(bf16[48,128]{1,0:T(8,128)(2,1)S(1)} %get-tuple-element.39), channel_id=1, source_target_pairs={{0,16},{2,18},{4,20},{6,22},{8,24},{10,26},{12,28},{14,30},{16,0},... | collective-permute-start | bytes 36872 | tf_op jit(solution)/shard_map/ppermute | solution.py:360
  66.1 1.7 %collective-permute-done.2.got_ref = bf16[48,128]{1,0:T(8,128)(2,1)S(1)} collective-permute-done((bf16[48,128]{1,0:T(8,128)(2,1)S(1)}, bf16[48,128]{1,0:T(8,128)(2,1)S(1)}, u32[]{:S(2)}, u32[]{:S(2)}) %collective-permute-start.2) | collective-permute-done | bytes 12320 | tf_op jit(solution)/shard_map/ppermute | solution.py:360
  67.8 0.1 join.1
  67.9 16.4 %all_to_all.35 = bf16[8,48,128]{2,1,0:T(8,128)(2,1)S(1)} all-to-all(bf16[8,48,128]{2,1,0:T(8,128)(2,1)S(1)} %bitcast.17), channel_id=1, replica_groups={{0,2,4,6,8,10,12,14},{16,18,20,22,24,26,28,30},{1,3,5,7,9,11,13,15},{17..., dimensions={0} | all-to-all | bytes 196608 | tf_op jit(solution)/shard_map/all_to_all | solution.py:356
  84.3 1.7 %level_3.1 = f32[8,64]{1,0:T(8,128)} custom-call(s32[8,8,128]{2,1,0:T(8,128)S(1)} %get-tuple-element.24.cols_ref, bf16[384,128]{1,0:T(8,128)(2,1)S(1)} %bitcast.16, f32[8,128]{1,0:T(8,128)S(1)} %get-tuple-element.40.total_ref), custom_call_target="tpu_custom_call" | custom-call | tf_op jit(solution)/shard_map/level_3/pallas_call | solution.py:341
Async XLA Ops:
  0.0 3.9 %copy-start = (bf16[8,64,512]{2,1,0:T(8,128)(2,1)S(1)}, bf16[8,64,512]{2,1,0:T(8,128)(2,1)}, u32[]{:S(2)}) copy-start(bf16[8,64,512]{2,1,0:T(8,128)(2,1)} %param.6) | copy-start | bytes 1572868
  0.0 3.9 %copy-start.4 = (s32[8]{0:T(128)S(1)}, s32[8]{0:T(128)}, u32[]{:S(2)}) copy-start(s32[8]{0:T(128)} %fine_map_ref.1) | copy-start | bytes 100
  2.1 1.8 %copy-start.2 = (s32[8,6]{1,0:T(8,128)S(1)}, s32[8,6]{1,0:T(8,128)}, u32[]{:S(2)}) copy-start(s32[8,6]{1,0:T(8,128)} %near_ref.1) | copy-start | bytes 580
  2.2 1.8 %copy-start.3 = (s32[1,3,8]{2,0,1:T(1,128)S(1)}, s32[1,3,8]{2,0,1:T(1,128)}, u32[]{:S(2)}) copy-start(s32[1,3,8]{2,0,1:T(1,128)} %param.9) | copy-start | bytes 292
  2.2 3.2 %collective-permute-start = (bf16[8,128]{1,0:T(8,128)(2,1)S(1)}, bf16[8,128]{1,0:T(8,128)(2,1)S(1)}, u32[]{:S(2)}, u32[]{:S(2)}) collective-permute-start(bf16[8,128]{1,0:T(8,128)(2,1)S(1)} %get-tuple-element.26.rounded_ref), channel_id=1, source_target_pairs={{0,1},{2,3},{4,5},{6,7},{8,9},{10,11},{12,13},{14,15},{16,17},{18,... | collective-permute-start | bytes 6152 | tf_op jit(solution)/shard_map/ppermute | solution.py:380
  4.0 1.4 %copy-start.1 = (f32[8,64]{1,0:T(8,128)S(1)}, f32[8,64]{1,0:T(8,128)}, u32[]{:S(2)}) copy-start(f32[8,64]{1,0:T(8,128)} %resid_ref.1) | copy-start | bytes 6148
  5.7 6.6 %collective-permute-start.1 = (bf16[400,128]{1,0:T(8,128)(2,1)S(1)}, bf16[400,128]{1,0:T(8,128)(2,1)S(1)}, u32[]{:S(2)}, u32[]{:S(2)}) collective-permute-start(bf16[400,128]{1,0:T(8,128)(2,1)S(1)} %get-tuple-element.28), channel_id=1, source_target_pairs={{0,2},{2,0},{4,6},{6,4},{8,10},{10,8},{12,14},{14,12},{16,18},{18,... | collective-permute-start | bytes 307208 | tf_op jit(solution)/shard_map/ppermute | solution.py:360
  50.4 17.4 %collective-permute-start.2 = (bf16[48,128]{1,0:T(8,128)(2,1)S(1)}, bf16[48,128]{1,0:T(8,128)(2,1)S(1)}, u32[]{:S(2)}, u32[]{:S(2)}) collective-permute-start(bf16[48,128]{1,0:T(8,128)(2,1)S(1)} %get-tuple-element.39), channel_id=1, source_target_pairs={{0,16},{2,18},{4,20},{6,22},{8,24},{10,26},{12,28},{14,30},{16,0},... | collective-permute-start | bytes 36872 | tf_op jit(solution)/shard_map/ppermute | solution.py:360
